TPU v7x, 256 devices: a whole 4x4x8 slice. The times are simulated.
256 devices in a mesh: rows: 32 (over z, x), cols: 8 (over y, core).
Axes of the slice: x: 4, y: 4, z: 8, core: 2. Of those that a mesh axis runs over, the one named last changes fastest.
Arguments:
- image: bfloat16 [512, 1536, 192], P('rows', 'cols'), may hold values from -6 to 6
- conv_kernel: float32 [7, 7, 192], replicated, may hold values from -0.875 to 0.875
- conv_bias: float32 [192], replicated, may hold values from -3 to 3
- norm_gain: float32 [192], replicated, may hold values from 0.5 to 1.5
- norm_bias: float32 [192], replicated, may hold values from -3 to 3
- in_weight: bfloat16 [192, 768], replicated, may hold values from -0.4375 to 0.4375
- in_bias: float32 [768], replicated, may hold values from -3 to 3
- out_weight: bfloat16 [768, 192], replicated, may hold values from -0.21875 to 0.21875
- out_bias: float32 [192], replicated, may hold values from -3 to 3
- layer_scale: float32 [192], replicated, may hold values from 0.5 to 1.5
- cotangent: bfloat16 [512, 1536, 192], P('rows', 'cols'), may hold values from -6 to 6
Outputs:
- output: bfloat16 [512, 1536, 192], P('rows', 'cols')
- grad_image: bfloat16 [512, 1536, 192], P('rows', 'cols')
- grad_kernel: float32 [7, 7, 192], replicated
- grad_conv_bias: float32 [192], replicated
- grad_gain: float32 [192], replicated
- grad_norm_bias: float32 [192], replicated
- grad_in_weight: float32 [192, 768], P(None, 'rows')
- grad_in_bias: float32 [768], P('rows')
- grad_out_weight: float32 [768, 192], P('rows')
- grad_out_bias: float32 [192], replicated
- grad_scale: float32 [192], replicated
All inputs are finite; a program needn't handle non-finite values.
Results may differ from a plain program's by a relative error of at most 0.0062.
Values may be sent and summed in bfloat16 or wider, within the bound.
A program may use at most 192 MiB of HBM per device.

v0:
```python
import math

import jax
import jax.numpy as jnp
from jax import lax
from jax.sharding import PartitionSpec as P


def padded_2(shard, sides, width):
    for axis, dim in sides:
        peers, length = (lax.axis_size(axis), shard.shape[dim])
        up = [(i, (i + 1) % peers) for i in range(peers - 1)]
        down = [(j, i) for i, j in up]
        last = lax.slice_in_dim(shard, length - width, length, axis=dim)
        first = lax.slice_in_dim(shard, 0, width, axis=dim)
        before = lax.ppermute(last, axis, up)
        after = lax.ppermute(first, axis, down)
        shard = jnp.concatenate([before, shard, after], axis=dim)
    return shard


def gelu_parts(hidden):
    normal_cdf = 0.5 * (1.0 + jax.scipy.special.erf(hidden * 0.7071067811865476))
    normal_pdf = jnp.exp(-0.5 * hidden * hidden) * 0.3989422804014327
    return (hidden * normal_cdf, normal_cdf + hidden * normal_pdf)


def depthwise(padded, conv_kernel, n_rows, n_cols):
    accum = jnp.zeros((n_rows, n_cols, conv_kernel.shape[2]), jnp.float32)
    for row_tap in range(7):
        for col_tap in range(7):
            shifted = padded[row_tap : row_tap + n_rows, col_tap : col_tap + n_cols].astype(
                jnp.float32
            )
            accum = accum + shifted * conv_kernel[row_tap, col_tap]
    return accum


def transposed(d_padded, conv_kernel, n_rows, n_cols):
    accum = jnp.zeros((n_rows, n_cols, conv_kernel.shape[2]), jnp.float32)
    for row_tap in range(7):
        for col_tap in range(7):
            shifted = d_padded[
                6 - row_tap : 6 - row_tap + n_rows, 6 - col_tap : 6 - col_tap + n_cols
            ].astype(jnp.float32)
            accum = accum + shifted * conv_kernel[row_tap, col_tap]
    return accum


def layer_pass(
    padded,
    cotangent,
    conv_kernel,
    conv_bias,
    norm_gain,
    norm_bias,
    in_weight,
    in_bias,
    out_weight,
    out_bias,
    layer_scale,
):
    n_rows, n_cols, channels = cotangent.shape
    pixels = n_rows * n_cols
    hidden_units = in_weight.shape[1]
    conv_out = depthwise(padded, conv_kernel, n_rows, n_cols) + conv_bias
    average = jnp.mean(conv_out, axis=-1, keepdims=True)
    centred = conv_out - average
    inv_std = lax.rsqrt(jnp.mean(centred * centred, axis=-1, keepdims=True) + 1e-06)
    unit_norm = centred * inv_std
    normed = (unit_norm * norm_gain + norm_bias).astype(jnp.bfloat16)
    hidden = (
        jnp.dot(normed.reshape(pixels, channels), in_weight, preferred_element_type=jnp.float32)
        + in_bias
    )
    act_full, gelu_slope = gelu_parts(hidden)
    activation = act_full.astype(jnp.bfloat16)
    branch = jnp.dot(activation, out_weight, preferred_element_type=jnp.float32) + out_bias
    centre = padded[3 : 3 + n_rows, 3 : 3 + n_cols].astype(jnp.float32).reshape(pixels, channels)
    output = (centre + layer_scale * branch).astype(jnp.bfloat16).reshape(n_rows, n_cols, channels)
    cot_full = cotangent.astype(jnp.float32).reshape(pixels, channels)
    scaled = (cot_full * layer_scale).astype(jnp.bfloat16)
    d_act = lax.dot_general(
        scaled, out_weight, (((1,), (1,)), ((), ())), preferred_element_type=jnp.float32
    )
    d_hidden_full = d_act * gelu_slope
    d_hidden = d_hidden_full.astype(jnp.bfloat16)
    d_normed = lax.dot_general(
        d_hidden, in_weight, (((1,), (1,)), ((), ())), preferred_element_type=jnp.float32
    )
    d_normed = d_normed.reshape(n_rows, n_cols, channels)
    d_unit = d_normed * norm_gain
    d_conv = (
        d_unit
        - jnp.mean(d_unit, axis=-1, keepdims=True)
        - unit_norm * jnp.mean(d_unit * unit_norm, axis=-1, keepdims=True)
    ) * inv_std
    shape_c = (n_rows, n_cols, channels)
    shape_h = (n_rows, n_cols, hidden_units)
    return (
        output,
        d_conv,
        unit_norm,
        normed,
        activation.reshape(shape_h),
        scaled.reshape(shape_c),
        d_hidden.reshape(shape_h),
        d_hidden_full.reshape(shape_h),
        d_normed,
        branch.reshape(shape_c),
        cot_full.reshape(shape_c),
    )


def partials(results, padded, offset, n_rows, n_cols, layer_scale):
    (
        output,
        d_conv,
        unit_norm,
        normed,
        activation,
        scaled,
        d_hidden,
        d_hidden_full,
        d_normed,
        branch,
        cot_full,
    ) = results

    def interior(array):
        return array.reshape(n_rows * n_cols, array.shape[2])

    tap_sums = []
    for row_tap in range(7):
        for col_tap in range(7):
            shifted = padded[
                offset + row_tap : offset + row_tap + n_rows,
                offset + col_tap : offset + col_tap + n_cols,
            ].astype(jnp.float32)
            tap_sums.append(jnp.sum(shifted * d_conv, axis=(0, 1)))
    g_kernel = jnp.stack(tap_sums).reshape(7, 7, d_conv.shape[2])
    g_conv_bias = jnp.sum(d_conv, axis=(0, 1))
    g_gain = jnp.sum(interior(d_normed) * interior(unit_norm), axis=0)
    g_norm_bias = jnp.sum(interior(d_normed), axis=0)
    g_in_weight = lax.dot_general(
        interior(normed),
        interior(d_hidden),
        (((0,), (0,)), ((), ())),
        preferred_element_type=jnp.float32,
    )
    g_in_bias = jnp.sum(interior(d_hidden_full), axis=0)
    g_out_weight = lax.dot_general(
        interior(activation),
        interior(scaled),
        (((0,), (0,)), ((), ())),
        preferred_element_type=jnp.float32,
    )
    g_out_bias = jnp.sum(interior(cot_full), axis=0) * layer_scale
    g_scale = jnp.sum(interior(cot_full) * interior(branch), axis=0)
    return (
        g_kernel,
        g_conv_bias,
        g_gain,
        g_norm_bias,
        g_in_weight,
        g_in_bias,
        g_out_weight,
        g_out_bias,
        g_scale,
    )


def body(
    image,
    conv_kernel,
    conv_bias,
    norm_gain,
    norm_bias,
    in_weight,
    in_bias,
    out_weight,
    out_bias,
    layer_scale,
    cotangent,
):
    n_rows, n_cols, channels = image.shape
    padded = padded_2(image, (("rows", 0), ("cols", 1)), 3)
    results = layer_pass(
        padded,
        cotangent,
        conv_kernel,
        conv_bias,
        norm_gain,
        norm_bias,
        in_weight,
        in_bias,
        out_weight,
        out_bias,
        layer_scale,
    )
    output = results[0]
    d_padded = padded_2(results[1].astype(jnp.bfloat16), (("rows", 0), ("cols", 1)), 3)
    grad_terms = partials(results, padded, 0, n_rows, n_cols, layer_scale)
    grad_image = (
        cotangent.astype(jnp.float32) + transposed(d_padded, conv_kernel, n_rows, n_cols)
    ).astype(jnp.bfloat16)
    (
        g_kernel,
        g_conv_bias,
        g_gain,
        g_norm_bias,
        g_in_weight,
        g_in_bias,
        g_out_weight,
        g_out_bias,
        g_scale,
    ) = grad_terms
    small_sums = lax.psum(
        (g_kernel, g_conv_bias, g_gain, g_norm_bias, g_out_bias, g_scale), ("rows", "cols")
    )
    band_sums = lax.psum((g_in_weight, g_in_bias, g_out_weight), "cols")
    shares = (
        lax.psum_scatter(band_sums[0], "rows", scatter_dimension=1, tiled=True),
        lax.psum_scatter(band_sums[1], "rows", scatter_dimension=0, tiled=True),
        lax.psum_scatter(band_sums[2], "rows", scatter_dimension=0, tiled=True),
    )
    factor = 1.0 / math.sqrt(n_rows * lax.axis_size("rows") * n_cols * lax.axis_size("cols"))
    return (
        output,
        grad_image,
        small_sums[0] * factor,
        small_sums[1] * factor,
        small_sums[2] * factor,
        small_sums[3] * factor,
        shares[0] * factor,
        shares[1] * factor,
        shares[2] * factor,
        small_sums[4] * factor,
        small_sums[5] * factor,
    )


def solution(mesh):
    placed = (
        P("rows", "cols", None),
        P(),
        P(),
        P(),
        P(),
        P(),
        P(),
        P(),
        P(),
        P(),
        P("rows", "cols", None),
    )
    return jax.shard_map(
        body,
        mesh=mesh,
        in_specs=placed,
        out_specs=(
            P("rows", "cols", None),
            P("rows", "cols", None),
            P(),
            P(),
            P(),
            P(),
            P(None, "rows"),
            P("rows"),
            P("rows", None),
            P(),
            P(),
        ),
        check_vma=False,
    )
```

profile of v0, /device:TPU:1, one launch (start us, length us, event | category | flops | bytes accessed | tf_op | source)
XLA Modules:
  0.0 616.0 jit_solution(3957431771738114136)
XLA Ops:
  8.5 4.0 collective-permute-start
  18.6 3.3 collective-permute-done.1
  23.3 4.9 collective-permute-start.2
  30.6 2.8 copy.34
  33.5 2.8 copy.32
  37.9 34.4 %fusion.152 = (f32[16,192]{1,0:T(8,128)S(1)}, f32[16,192,192]{2,1,0:T(8,128)S(1)}) fusion(f32[192]{0:T(256)S(1)} %copy-done.94, f32[192]{0:T(256)} %bitcast.49, bf16[22,3,192]{2,1,0:T(4,128)(2,1)S(1)} %collective-permute-done.3, bf16[22,192,192]{2,1,0:T(8,128)(2,1)S(1)} %get-tuple-element.125, f32[192]{0:T(256)} %bitcast.48, f32[192]{0:T(256)S(1)} %bitcast.127, ...), kind=kLoop, calls=%fused_computation.342 | loop fusion | flops 161608704 | bytes 12340224 | tf_op jit(solution)/shard_map/reduce_sum | solution.py:67
  73.5 2.7 add_convert_fusion.1
  76.2 3.4 copy.36
  79.6 5.4 multiply_convert_fusion
  85.0 6.1 fusion.160
  91.1 2.2 copy-done.13
  93.2 3.0 fusion.102
  96.2 6.2 %fusion.151 = (f32[192]{0:T(256)S(1)}, f32[192]{0:T(256)S(1)}, f32[3072]{0:T(1024)S(1)}, f32[3072,192]{0,1:T(8,128)}) fusion(f32[3072,192]{0,1:T(8,128)} %copy.36, f32[192]{0:T(256)S(1)} %copy-done.16, bf16[192,768]{1,0:T(8,128)(2,1)S(1)} %copy-done, bf16[3072,768]{1,0:T(8,128)(2,1)} %copy-done.13), kind=kOutput, calls=%fused_computation.341 | convolution fusion | flops 908915328 | bytes 9746688 | tf_op jit(solution)/shard_map/dot_general | solution.py:88
  102.4 3.4 copy.35
  105.8 3.5 multiply_reduce_fusion.1
  109.4 7.9 %fusion.100 = (f32[192]{0:T(256)S(1)}, f32[192]{0:T(256)S(1)}, f32[192]{0:T(256)S(1)}, f32[192]{0:T(256)S(1)}, f32[192]{0:T(256)S(1)}, /*index=5*/f32[192]{0:T(256)S(1)}, f32[192]{0:T(256)S(1)}, f32[16,192,192]{2,1,0:T(8,128)S(1)}) fusion(bf16[22,3,192]{2,1,0:T(4,128)(2,1)S(1)} %collective-permute-done.3, bf16[22,192,192]{2,1,0:T(8,128)(2,1)S(1)} %get-tuple-element.125, ...), kind=kLoop, calls=%fused_computation.240 | loop fusion | flops 24771264 | bytes 8768256 | tf_op jit(solution)/shard_map/reduce_sum | solution.py:140
  117.3 2.8 fusion.97
  120.2 4.3 fusion.86
  124.4 3.6 fusion.82
  128.1 4.3 fusion.50
  132.3 3.6 fusion.46
  136.0 4.0 fusion.36
  139.9 4.5 fusion.96
  144.7 5.7 multiply_reduce_fusion.3
  150.4 83.3 %all-reduce.1 = (f32[7,7,192]{2,1,0:T(8,128)S(1)}, f32[192]{0:T(256)}, f32[192]{0:T(256)S(1)}, f32[192]{0:T(256)S(1)}, f32[192]{0:T(256)S(1)}, /*index=5*/f32[192]{0:T(256)S(1)}) all-reduce(f32[7,7,192]{2,1,0:T(8,128)S(1)} %reshape.81, f32[192]{0:T(256)S(1)} %get-tuple-element.84, ...), channel_id=1, replica_groups=mesh['rows'=32,'cols'=8] {'rows','cols'}, use_global_device_ids=true, to_apply=%region_53.0 | all-reduce | flops 10368 | bytes 82944 | tf_op jit(solution)/shard_map/psum | solution.py:218
  239.1 5.5 fusion.150
  246.4 4.6 collective-permute-start.6
  255.7 57.2 %all-reduce = f32[768]{0:T(1024)S(1)} all-reduce(f32[768]{0:T(1024)} %get-tuple-element.178), channel_id=3, replica_groups=mesh['rows'=32,'cols'=8] {'rows'}, use_global_device_ids=true, to_apply=%region_64.0.clone | all-reduce | flops 768 | bytes 6144
  315.4 35.3 %add_convert_fusion = bf16[16,192,192]{2,1,0:T(8,128)(2,1)} fusion(bf16[16,192,192]{2,1,0:T(8,128)(2,1)S(1)} %copy-done.8, bf16[3,192,192]{2,1,0:T(8,128)(2,1)S(1)} %collective-permute-done.4, bf16[3,192,192]{2,1,0:T(8,128)(2,1)} %copy-done.14, bf16[22,195,192]{2,1,0:T(8,128)(2,1)S(1)} %get-tuple-element.110, ...), kind=kLoop, calls=%fused_computation.242 | loop fusion | flops 91422720 | bytes 53564160 | tf_op jit(solution)/shard_map/convert_element_type | solution.py:206
  350.7 10.6 %reduce-scatter.3.cloned.1.call-done = f32[192,24]{0,1:T(8,128)} async-done(((f32[192,768]{0,1:T(8,128)}), f32[192,24]{0,1:T(8,128)}) %reduce-scatter.3.cloned.1.call-update) | async-done | bytes 18448 | tf_op jit(solution)/shard_map/reduce_scatter | solution.py:223
  361.3 218.9 %reduce-scatter.5.cloned.1.call-done = f32[24,192]{1,0:T(8,128)} async-done(((f32[768,192]{1,0:T(8,128)}), f32[24,192]{1,0:T(8,128)}) %reduce-scatter.5.cloned.1.call-update) | async-done | bytes 18448 | tf_op jit(solution)/shard_map/reduce_scatter | solution.py:225
  580.2 27.2 %all-reduce.2 = (f32[192,24]{0,1:T(8,128)S(1)}, f32[24]{0:T(128)S(1)}, f32[24,192]{1,0:T(8,128)S(1)}) all-reduce(f32[192,24]{0,1:T(8,128)} %reduce-scatter.3.cloned.1.call-done, f32[24]{0:T(128)S(1)} %dynamic-slice.1, f32[24,192]{1,0:T(8,128)} %reduce-scatter.5.cloned.1.call-done), channel_id=1, replica_groups=mesh['rows'=32,'cols'=8] {'cols'}, use_global_device_ids=true, to_apply=%region_60.0 | all-reduce | flops 9240 | bytes 73920 | tf_op jit(solution)/shard_map/psum | solution.py:221
  (240 shorter events, 28.5 us)
Async XLA Ops:
  7.2 72.4 %copy-start = (bf16[192,768]{1,0:T(8,128)(2,1)S(1)}, bf16[192,768]{1,0:T(8,128)(2,1)}, u32[]{:S(2)}) copy-start(bf16[192,768]{1,0:T(8,128)(2,1)} %param.16) | copy-start | bytes 884740
  7.2 354.1 %reduce-scatter.3.cloned.1.call-start = ((), (), s32[]{:S(2)}) async-start(), calls=%async_computation.2 | async-start | bytes 811008 | tf_op jit(solution)/shard_map/reduce_scatter | solution.py:223
  8.5 9.6 %collective-permute-start = (bf16[3,192,192]{2,1,0:T(8,128)(2,1)S(1)}, bf16[3,192,192]{2,1,0:T(8,128)(2,1)S(1)}, u32[]{:S(2)}, u32[]{:S(2)}) collective-permute-start(bf16[3,192,192]{2,1,0:T(8,128)(2,1)S(1)} %get-tuple-element.121), channel_id=1, source_target_pairs={{0,8},{8,16},{16,24},{24,32},{32,40},{40,48},{48,56},{56,64},{64,7... | collective-permute-start | bytes 663560 | tf_op jit(solution)/shard_map/ppermute | solution.py:16
  12.4 9.5 %collective-permute-start.1 = (bf16[3,192,192]{2,1,0:T(8,128)(2,1)S(1)}, bf16[3,192,192]{2,1,0:T(8,128)(2,1)S(1)}, u32[]{:S(2)}, u32[]{:S(2)}) collective-permute-start(bf16[3,192,192]{2,1,0:T(8,128)(2,1)S(1)} %get-tuple-element.120), channel_id=1, source_target_pairs={{8,0},{16,8},{24,16},{32,24},{40,32},{48,40},{56,48},{64,56},{72,6... | collective-permute-start | bytes 663560 | tf_op jit(solution)/shard_map/ppermute | solution.py:17
  14.7 22.8 %copy-start.19 = (f32[1,1,192]{2,1,0:T(1,128)}, f32[1,1,192]{2,1,0:T(1,128)S(1)}, u32[]{:S(2)}) copy-start(f32[1,1,192]{2,1,0:T(1,128)S(1)} %get-tuple-element.134) | copy-start | bytes 2308
  14.7 22.8 %copy-start.21 = (f32[1,1,192]{2,1,0:T(1,128)}, f32[1,1,192]{2,1,0:T(1,128)S(1)}, u32[]{:S(2)}) copy-start(f32[1,1,192]{2,1,0:T(1,128)S(1)} %get-tuple-element.135) | copy-start | bytes 2308
  14.7 22.8 %copy-start.23 = (f32[1,1,192]{2,1,0:T(1,128)}, f32[1,1,192]{2,1,0:T(1,128)S(1)}, u32[]{:S(2)}) copy-start(f32[1,1,192]{2,1,0:T(1,128)S(1)} %get-tuple-element.136) | copy-start | bytes 2308
  14.8 22.8 %copy-start.25 = (f32[1,1,192]{2,1,0:T(1,128)}, f32[1,1,192]{2,1,0:T(1,128)S(1)}, u32[]{:S(2)}) copy-start(f32[1,1,192]{2,1,0:T(1,128)S(1)} %get-tuple-element.137) | copy-start | bytes 2308
  14.8 22.8 %copy-start.27 = (f32[1,1,192]{2,1,0:T(1,128)}, f32[1,1,192]{2,1,0:T(1,128)S(1)}, u32[]{:S(2)}) copy-start(f32[1,1,192]{2,1,0:T(1,128)S(1)} %get-tuple-element.138) | copy-start | bytes 2308
  14.8 22.8 %copy-start.29 = (f32[1,1,192]{2,1,0:T(1,128)}, f32[1,1,192]{2,1,0:T(1,128)S(1)}, u32[]{:S(2)}) copy-start(f32[1,1,192]{2,1,0:T(1,128)S(1)} %get-tuple-element.139) | copy-start | bytes 2308
  14.8 22.8 %copy-start.31 = (f32[1,1,192]{2,1,0:T(1,128)}, f32[1,1,192]{2,1,0:T(1,128)S(1)}, u32[]{:S(2)}) copy-start(f32[1,1,192]{2,1,0:T(1,128)S(1)} %get-tuple-element.140) | copy-start | bytes 2308
  14.8 22.8 %copy-start.33 = (f32[1,1,192]{2,1,0:T(1,128)}, f32[1,1,192]{2,1,0:T(1,128)S(1)}, u32[]{:S(2)}) copy-start(f32[1,1,192]{2,1,0:T(1,128)S(1)} %get-tuple-element.141) | copy-start | bytes 2308
  14.8 22.8 %copy-start.35 = (f32[1,1,192]{2,1,0:T(1,128)}, f32[1,1,192]{2,1,0:T(1,128)S(1)}, u32[]{:S(2)}) copy-start(f32[1,1,192]{2,1,0:T(1,128)S(1)} %get-tuple-element.142) | copy-start | bytes 2308
  14.8 22.8 %copy-start.37 = (f32[1,1,192]{2,1,0:T(1,128)}, f32[1,1,192]{2,1,0:T(1,128)S(1)}, u32[]{:S(2)}) copy-start(f32[1,1,192]{2,1,0:T(1,128)S(1)} %get-tuple-element.143) | copy-start | bytes 2308
  14.8 22.8 %copy-start.39 = (f32[1,1,192]{2,1,0:T(1,128)}, f32[1,1,192]{2,1,0:T(1,128)S(1)}, u32[]{:S(2)}) copy-start(f32[1,1,192]{2,1,0:T(1,128)S(1)} %get-tuple-element.144) | copy-start | bytes 2308
  15.9 21.8 %copy-start.41 = (f32[1,1,192]{2,1,0:T(1,128)}, f32[1,1,192]{2,1,0:T(1,128)S(1)}, u32[]{:S(2)}) copy-start(f32[1,1,192]{2,1,0:T(1,128)S(1)} %get-tuple-element.145) | copy-start | bytes 2308
  15.9 21.8 %copy-start.43 = (f32[1,1,192]{2,1,0:T(1,128)}, f32[1,1,192]{2,1,0:T(1,128)S(1)}, u32[]{:S(2)}) copy-start(f32[1,1,192]{2,1,0:T(1,128)S(1)} %get-tuple-element.146) | copy-start | bytes 2308
  15.9 21.8 %copy-start.45 = (f32[1,1,192]{2,1,0:T(1,128)}, f32[1,1,192]{2,1,0:T(1,128)S(1)}, u32[]{:S(2)}) copy-start(f32[1,1,192]{2,1,0:T(1,128)S(1)} %get-tuple-element.147) | copy-start | bytes 2308
  15.9 21.8 %copy-start.47 = (f32[1,1,192]{2,1,0:T(1,128)}, f32[1,1,192]{2,1,0:T(1,128)S(1)}, u32[]{:S(2)}) copy-start(f32[1,1,192]{2,1,0:T(1,128)S(1)} %get-tuple-element.148) | copy-start | bytes 2308
  15.9 21.8 %copy-start.49 = (f32[1,1,192]{2,1,0:T(1,128)}, f32[1,1,192]{2,1,0:T(1,128)S(1)}, u32[]{:S(2)}) copy-start(f32[1,1,192]{2,1,0:T(1,128)S(1)} %get-tuple-element.149) | copy-start | bytes 2308
  15.9 21.8 %copy-start.51 = (f32[1,1,192]{2,1,0:T(1,128)}, f32[1,1,192]{2,1,0:T(1,128)S(1)}, u32[]{:S(2)}) copy-start(f32[1,1,192]{2,1,0:T(1,128)S(1)} %get-tuple-element.150) | copy-start | bytes 2308
  15.9 21.8 %copy-start.53 = (f32[1,1,192]{2,1,0:T(1,128)}, f32[1,1,192]{2,1,0:T(1,128)S(1)}, u32[]{:S(2)}) copy-start(f32[1,1,192]{2,1,0:T(1,128)S(1)} %get-tuple-element.151) | copy-start | bytes 2308
  23.3 14.2 %collective-permute-start.2 = (bf16[22,3,192]{2,1,0:T(4,128)(2,1)S(1)}, bf16[22,3,192]{2,1,0:T(4,128)(2,1)S(1)}, u32[]{:S(2)}, u32[]{:S(2)}) collective-permute-start(bf16[22,3,192]{2,1,0:T(4,128)(2,1)S(1)} %get-tuple-element.113), channel_id=1, source_target_pairs={{0,1},{1,2},{2,3},{3,4},{4,5},{5,6},{6,7},{8,9},{9,10},{10,11},{11... | collective-permute-start | bytes 76040 | tf_op jit(solution)/shard_map/ppermute | solution.py:16
  28.2 9.3 %collective-permute-start.3 = (bf16[22,3,192]{2,1,0:T(4,128)(2,1)S(1)}, bf16[22,3,192]{2,1,0:T(4,128)(2,1)S(1)}, u32[]{:S(2)}, u32[]{:S(2)}) collective-permute-start(bf16[22,3,192]{2,1,0:T(4,128)(2,1)S(1)} %get-tuple-element.114), channel_id=1, source_target_pairs={{1,0},{2,1},{3,2},{4,3},{5,4},{6,5},{7,6},{9,8},{10,9},{11,10},{12... | collective-permute-start | bytes 76040 | tf_op jit(solution)/shard_map/ppermute | solution.py:17
  144.6 435.6 %reduce-scatter.5.cloned.1.call-start = ((), (), s32[]{:S(2)}) async-start(), calls=%async_computation.3 | async-start | bytes 811008 | tf_op jit(solution)/shard_map/reduce_scatter | solution.py:225
  144.7 89.6 %copy-start.8 = (bf16[16,192,192]{2,1,0:T(8,128)(2,1)S(1)}, bf16[16,192,192]{2,1,0:T(8,128)(2,1)}, u32[]{:S(2)}) copy-start(bf16[16,192,192]{2,1,0:T(8,128)(2,1)} %get-tuple-element.106) | copy-start | bytes 3538948
  235.2 10.0 %collective-permute-start.4 = (bf16[3,192,192]{2,1,0:T(8,128)(2,1)}, bf16[3,192,192]{2,1,0:T(8,128)(2,1)S(1)}, u32[]{:S(2)}, u32[]{:S(2)}) collective-permute-start(bf16[3,192,192]{2,1,0:T(8,128)(2,1)} %get-tuple-element.116), channel_id=1, source_target_pairs={{0,8},{8,16},{16,24},{24,32},{32,40},{40,48},{48,56},{56,64},{64,7... | collective-permute-start | bytes 663560 | tf_op jit(solution)/shard_map/ppermute | solution.py:16
  237.2 9.1 %collective-permute-start.5 = (bf16[3,192,192]{2,1,0:T(8,128)(2,1)}, bf16[3,192,192]{2,1,0:T(8,128)(2,1)S(1)}, u32[]{:S(2)}, u32[]{:S(2)}) collective-permute-start(bf16[3,192,192]{2,1,0:T(8,128)(2,1)} %get-tuple-element.115), channel_id=1, source_target_pairs={{8,0},{16,8},{24,16},{32,24},{40,32},{48,40},{56,48},{64,56},{72,6... | collective-permute-start | bytes 663560 | tf_op jit(solution)/shard_map/ppermute | solution.py:17
  246.3 68.7 %copy-start.14 = (bf16[3,192,192]{2,1,0:T(8,128)(2,1)}, bf16[3,192,192]{2,1,0:T(8,128)(2,1)S(1)}, u32[]{:S(2)}) copy-start(bf16[3,192,192]{2,1,0:T(8,128)(2,1)S(1)} %collective-permute-done.5) | copy-start | bytes 663556
  246.4 66.9 %collective-permute-start.6 = (bf16[22,3,192]{2,1,0:T(4,128)(2,1)S(1)}, bf16[22,3,192]{2,1,0:T(4,128)(2,1)S(1)}, u32[]{:S(2)}, u32[]{:S(2)}) collective-permute-start(bf16[22,3,192]{2,1,0:T(4,128)(2,1)S(1)} %get-tuple-element.111), channel_id=1, source_target_pairs={{1,0},{2,1},{3,2},{4,3},{5,4},{6,5},{7,6},{9,8},{10,9},{11,10},{12... | collective-permute-start | bytes 76040 | tf_op jit(solution)/shard_map/ppermute | solution.py:17
  251.0 62.4 %collective-permute-start.7 = (bf16[22,3,192]{2,1,0:T(4,128)(2,1)S(1)}, bf16[22,3,192]{2,1,0:T(4,128)(2,1)S(1)}, u32[]{:S(2)}, u32[]{:S(2)}) collective-permute-start(bf16[22,3,192]{2,1,0:T(4,128)(2,1)S(1)} %get-tuple-element.112), channel_id=1, source_target_pairs={{0,1},{1,2},{2,3},{3,4},{4,5},{5,6},{6,7},{8,9},{9,10},{10,11},{11... | collective-permute-start | bytes 76040 | tf_op jit(solution)/shard_map/ppermute | solution.py:16
  315.4 293.8 %copy-start.1 = (bf16[192,768]{1,0:T(8,128)(2,1)S(1)}, bf16[192,768]{1,0:T(8,128)(2,1)}, u32[]{:S(2)}) copy-start(bf16[192,768]{1,0:T(8,128)(2,1)} %param.16) | copy-start | bytes 884740
  (75 other events, 584.6 us)
Sparse Core Ops, SparseCore 0:
  144.8 216.5 reduce-scatter.2
  365.1 215.0 reduce-scatter.4
where the time goes:
time: 618 us; the launch traced here: 616 us
  waiting for transfers between devices  235 us (38%)
  blocking collectives  168 us (27%)
  other arithmetic  119 us (19%)
  matrix products  31.8 us (5%)
  local copies, waits for them, and re-layouts  24.9 us (4%)
  starting transfers between devices  21.9 us (4%)
  between operations  16.3 us (3%)
    reduce_scatter x1, waiting for transfers between devices, body(): lax.psum_scatter(band_sums[2], 'rows', scatter_dimension=0, tiled=True)  219 us
    psum x1, blocking collectives, body(): lax.psum((g_kernel, g_conv_bias, g_gain, g_norm_bias, g_out_bias, g_scale...  83.3 us
    unnamed x1, blocking collectives  57.2 us
    convert_element_type x1, other arithmetic, body(): grad_image = (cotangent.astype(jnp.float32) + transposed(d_padded, conv_k...  35.3 us
    reduce_sum x8, other arithmetic, partials(): tap_sums.append(jnp.sum(shifted * d_conv, axis=(0, 1)))  35 us
    reduce_sum x1, other arithmetic, layer_pass(): average = jnp.mean(conv_out, axis=-1, keepdims=True)  34.4 us
    psum x1, blocking collectives, body(): band_sums = lax.psum((g_in_weight, g_in_bias, g_out_weight), 'cols')  27.2 us
    ppermute x4, starting transfers between devices, padded_2(): before = lax.ppermute(last, axis, up)  12.8 us
  transfers between devices with their start and end apart: 10, of which 5 were waited for; matrix products, arithmetic and copies ran while one was open for 10% of the time, Pallas kernels for 0%

commit v1 on v0

--- a/solution.py
+++ b/solution.py
@@ -1,8 +1,11 @@
+import functools
 import math
 
 import jax
 import jax.numpy as jnp
 from jax import lax
+from jax.experimental import pallas as pl
+from jax.experimental.pallas import tpu as pltpu
 from jax.sharding import PartitionSpec as P
 
 
@@ -168,6 +171,286 @@
         g_out_bias,
         g_scale,
     )
+
+
+MESH = pl.DeviceIdType.MESH
+SHARE = 24
+
+
+def reduce_kernel(
+    factor,
+    w_ref,
+    s_ref,
+    wout_ref,
+    sout_ref,
+    core_tx,
+    core_rx,
+    score_rx,
+    row_tx,
+    srow_tx,
+    row_rx,
+    srow_rx,
+    col_rx,
+    scol_rx,
+    gat_tx,
+    gat_rx,
+    core_send,
+    core_recv,
+    row_send,
+    row_recv,
+    col_send,
+    col_recv,
+    gat_send,
+    gat_recv,
+):
+    row = lax.axis_index("rows")
+    col = lax.axis_index("cols")
+    core = lax.rem(col, 2)
+    pair = col - core
+    other = pair + 1 - core
+    half = row // 16
+    place = lax.rem(row, 16)
+    owner = half == core
+
+    barrier = pltpu.get_barrier_semaphore()
+
+    def greet_row(step, carry):
+        peer = lax.rem(row + step, 32)
+        pl.semaphore_signal(barrier, inc=1, device_id=(peer, col), device_id_type=MESH)
+        return carry
+
+    def greet_col(step, carry):
+        peer = lax.rem(col + step, 8)
+        pl.semaphore_signal(barrier, inc=1, device_id=(row, peer), device_id_type=MESH)
+        return carry
+
+    lax.fori_loop(1, 32, greet_row, 0)
+    lax.fori_loop(1, 8, greet_col, 0)
+
+    def share_of(index):
+        rows = w_ref[pl.ds(pl.multiple_of(index * SHARE, 8), SHARE), :]
+        return jnp.concatenate([rows[:, 0:128], rows[:, 128:256], rows[:, 256:384]], axis=0)
+
+    def pack_core(j, carry):
+        core_tx[j] = share_of(16 * (1 - core) + j).astype(jnp.bfloat16)
+        return carry
+
+    lax.fori_loop(0, 16, pack_core, 0)
+    pl.semaphore_wait(barrier, 38)
+
+    to_core = pltpu.make_async_remote_copy(
+        core_tx, core_rx, core_send.at[0], core_recv.at[0], device_id=(row, other), device_id_type=MESH
+    )
+    to_core_s = pltpu.make_async_remote_copy(
+        s_ref, score_rx, core_send.at[1], core_recv.at[1], device_id=(row, other), device_id_type=MESH
+    )
+    to_core.start()
+    to_core_s.start()
+    to_core.wait()
+    to_core_s.wait()
+
+    for j in range(16):
+        top, left = 8 * (j // 2), 128 * (j % 2)
+        srow_tx[j] = (
+            s_ref[top : top + 8, left : left + 128] + score_rx[top : top + 8, left : left + 128]
+        )
+
+    def row_copies(j):
+        return (
+            pltpu.make_async_remote_copy(
+                row_tx.at[j],
+                row_rx.at[row],
+                row_send.at[0, j],
+                row_recv.at[0, row],
+                device_id=(16 * core + j, col),
+                device_id_type=MESH,
+            ),
+            pltpu.make_async_remote_copy(
+                srow_tx.at[j],
+                srow_rx.at[row],
+                row_send.at[1, j],
+                row_recv.at[1, row],
+                device_id=(16 * core + j, col),
+                device_id_type=MESH,
+            ),
+        )
+
+    def pack_row(step, carry):
+        j = lax.rem(place + step, 16)
+        row_tx[j] = (share_of(16 * core + j) + core_rx[j].astype(jnp.float32)).astype(jnp.bfloat16)
+        return carry
+
+    def send_row(step, carry):
+        j = lax.rem(place + step, 16)
+
+        @pl.when(16 * core + j != row)
+        def _():
+            for copy in row_copies(j):
+                copy.start()
+
+        return carry
+
+    lax.fori_loop(0, 16, pack_row, 0)
+    lax.fori_loop(0, 16, send_row, 0)
+
+    def col_copies(step):
+        peer = lax.rem(col + step, 8)
+        return (
+            pltpu.make_async_remote_copy(
+                col_rx.at[col // 2],
+                col_rx.at[col // 2],
+                col_send.at[0, step],
+                col_recv.at[0, col // 2],
+                device_id=(row, peer),
+                device_id_type=MESH,
+            ),
+            pltpu.make_async_remote_copy(
+                scol_rx.at[col // 2],
+                scol_rx.at[col // 2],
+                col_send.at[1, step],
+                col_recv.at[1, col // 2],
+                device_id=(row, peer),
+                device_id_type=MESH,
+            ),
+        )
+
+    @pl.when(owner)
+    def _():
+        row_rx[row] = row_tx[place]
+        srow_rx[row] = srow_tx[place]
+
+        def wait_row(step, carry):
+            peer = lax.rem(row + step, 32)
+            pltpu.make_async_copy(row_tx.at[0], row_rx.at[peer], row_recv.at[0, peer]).wait()
+            pltpu.make_async_copy(srow_tx.at[0], srow_rx.at[peer], row_recv.at[1, peer]).wait()
+            return carry
+
+        lax.fori_loop(1, 32, wait_row, 0)
+
+        def add_row(i, carry):
+            return (carry[0] + row_rx[i].astype(jnp.float32), carry[1] + srow_rx[i])
+
+        total, s_total = lax.fori_loop(
+            0, 32, add_row, (jnp.zeros((72, 128), jnp.float32), jnp.zeros((8, 128), jnp.float32))
+        )
+        col_rx[col // 2] = total.astype(jnp.bfloat16)
+        scol_rx[col // 2] = s_total
+
+        def send_col(step, carry):
+            for copy in col_copies(step):
+                copy.start()
+            return carry
+
+        lax.fori_loop(1, 8, send_col, 0)
+
+    def wait_col(y, carry):
+        @pl.when(2 * y + half != col)
+        def _():
+            pltpu.make_async_copy(col_rx.at[y], col_rx.at[y], col_recv.at[0, y]).wait()
+            pltpu.make_async_copy(scol_rx.at[y], scol_rx.at[y], col_recv.at[1, y]).wait()
+
+        return carry
+
+    lax.fori_loop(0, 4, wait_col, 0)
+    block = (scol_rx[0] + scol_rx[1]) + (scol_rx[2] + scol_rx[3])
+    gat_tx[...] = block * factor
+    share = jnp.zeros((72, 128), jnp.float32)
+    for y in range(4):
+        share = share + col_rx[y].astype(jnp.float32)
+    share = share * factor
+
+    def gather_copy(step):
+        peer = 16 * half + lax.rem(place + step, 16)
+        return pltpu.make_async_remote_copy(
+            gat_tx,
+            gat_rx.at[place],
+            gat_send.at[step],
+            gat_recv.at[place],
+            device_id=(peer, col),
+            device_id_type=MESH,
+        )
+
+    def send_gather(step, carry):
+        gather_copy(step).start()
+        return carry
+
+    lax.fori_loop(1, 16, send_gather, 0)
+    for k in range(3):
+        wout_ref[:, 128 * k : 128 * (k + 1)] = share[SHARE * k : SHARE * (k + 1)]
+    gat_rx[place] = gat_tx[...]
+
+    def wait_gather(step, carry):
+        peer = lax.rem(place + step, 16)
+        pltpu.make_async_copy(gat_tx, gat_rx.at[peer], gat_recv.at[peer]).wait()
+        return carry
+
+    lax.fori_loop(1, 16, wait_gather, 0)
+    for j in range(16):
+        top, left = 8 * (j // 2), 128 * (j % 2)
+        sout_ref[top : top + 8, left : left + 128] = gat_rx[j]
+
+    def drain_row(step, carry):
+        j = lax.rem(place + step, 16)
+
+        @pl.when(16 * core + j != row)
+        def _():
+            for copy in row_copies(j):
+                copy.wait_send()
+
+        return carry
+
+    lax.fori_loop(0, 16, drain_row, 0)
+
+    @pl.when(owner)
+    def _():
+        def drain_col(step, carry):
+            for copy in col_copies(step):
+                copy.wait_send()
+            return carry
+
+        lax.fori_loop(1, 8, drain_col, 0)
+
+    def drain_gather(step, carry):
+        gather_copy(step).wait_send()
+        return carry
+
+    lax.fori_loop(1, 16, drain_gather, 0)
+
+
+def reduce_all(w_sum, s_sum, factor):
+    vmem = pl.BlockSpec(memory_space=pltpu.VMEM)
+    dma = pltpu.SemaphoreType.DMA
+    return pl.pallas_call(
+        functools.partial(reduce_kernel, factor),
+        out_shape=(
+            jax.ShapeDtypeStruct((SHARE, 384), jnp.float32),
+            jax.ShapeDtypeStruct((64, 256), jnp.float32),
+        ),
+        in_specs=[vmem, vmem],
+        out_specs=(vmem, vmem),
+        scratch_shapes=[
+            pltpu.VMEM((16, 72, 128), jnp.bfloat16),
+            pltpu.VMEM((16, 72, 128), jnp.bfloat16),
+            pltpu.VMEM((64, 256), jnp.float32),
+            pltpu.VMEM((16, 72, 128), jnp.bfloat16),
+            pltpu.VMEM((16, 8, 128), jnp.float32),
+            pltpu.VMEM((32, 72, 128), jnp.bfloat16),
+            pltpu.VMEM((32, 8, 128), jnp.float32),
+            pltpu.VMEM((4, 72, 128), jnp.bfloat16),
+            pltpu.VMEM((4, 8, 128), jnp.float32),
+            pltpu.VMEM((8, 128), jnp.float32),
+            pltpu.VMEM((16, 8, 128), jnp.float32),
+            dma((2,)),
+            dma((2,)),
+            dma((2, 16)),
+            dma((2, 32)),
+            dma((2, 8)),
+            dma((2, 4)),
+            dma((16,)),
+            dma((16,)),
+        ],
+        compiler_params=pltpu.CompilerParams(collective_id=0, has_side_effects=True),
+    )(w_sum, s_sum)
 
 
 def body(
@@ -215,28 +498,38 @@
         g_out_bias,
         g_scale,
     ) = grad_terms
-    small_sums = lax.psum(
-        (g_kernel, g_conv_bias, g_gain, g_norm_bias, g_out_bias, g_scale), ("rows", "cols")
-    )
-    band_sums = lax.psum((g_in_weight, g_in_bias, g_out_weight), "cols")
-    shares = (
-        lax.psum_scatter(band_sums[0], "rows", scatter_dimension=1, tiled=True),
-        lax.psum_scatter(band_sums[1], "rows", scatter_dimension=0, tiled=True),
-        lax.psum_scatter(band_sums[2], "rows", scatter_dimension=0, tiled=True),
-    )
     factor = 1.0 / math.sqrt(n_rows * lax.axis_size("rows") * n_cols * lax.axis_size("cols"))
+    hidden_units = in_weight.shape[1]
+    w_sum = jnp.concatenate([g_in_weight.T, g_out_weight], axis=1)
+    s_sum = jnp.concatenate(
+        [
+            g_kernel.reshape(49, channels),
+            g_conv_bias[None],
+            g_gain[None],
+            g_norm_bias[None],
+            g_out_bias[None],
+            g_scale[None],
+            g_in_bias.reshape(4, channels),
+        ],
+        axis=0,
+    )
+    s_sum = jnp.pad(s_sum, ((0, 6), (0, 64)))
+    w_share, s_all = reduce_all(w_sum, s_sum, factor)
+    s_all = s_all[:, :channels]
+    bias_all = s_all[54:58].reshape(hidden_units)
+    bias_share = lax.dynamic_slice(bias_all, (lax.axis_index("rows") * SHARE,), (SHARE,))
     return (
         output,
         grad_image,
-        small_sums[0] * factor,
-        small_sums[1] * factor,
-        small_sums[2] * factor,
-        small_sums[3] * factor,
-        shares[0] * factor,
-        shares[1] * factor,
-        shares[2] * factor,
-        small_sums[4] * factor,
-        small_sums[5] * factor,
+        s_all[:49].reshape(7, 7, channels),
+        s_all[49],
+        s_all[50],
+        s_all[51],
+        w_share[:, :channels].T,
+        bias_share,
+        w_share[:, channels:],
+        s_all[52],
+        s_all[53],
     )
 
 

time: 618 us -> 261 us (0.42)
  waiting for transfers between devices: 235 us -> 3.21 us
  blocking collectives: 168 us -> 0 us
  Pallas kernels: 0 us -> 42 us
  between operations: 16.3 us -> 2.38 us
  local copies, waits for them, and re-layouts: 24.9 us -> 34.6 us
  other arithmetic: 119 us -> 127 us
    reduce_scatter x2 -> x0, waiting for transfers between devices: 229 us -> none  [the longest x1 219 us: body(): lax.psum_scatter(band_sums[2], 'rows', scatter_dimension=0, tiled=True)]
    psum x2 -> x0, blocking collectives: 111 us -> none  [the longest x1 83.3 us: body(): lax.psum((g_kernel, g_conv_bias, g_gain, g_norm_bias, g_out_bias, g_scale...]
    unnamed x1 -> x0, blocking collectives: 57.2 us -> none
    pallas_call x0 -> x1, Pallas kernels: none -> 42 us  [reduce_all(): pl.pallas_call(functools.partial(reduce_kernel, factor), out_shape=(jax.S...]
    reduce_sum x8, other arithmetic: 35 us -> 42.4 us  [partials(): tap_sums.append(jnp.sum(shifted * d_conv, axis=(0, 1)))]
  transfers between devices with their start and end apart: 10 -> 8, of which waited for: 5 -> 1; matrix products, arithmetic and copies ran while one was open for 10% -> 21% of each run, Pallas kernels for 0% -> 16%
where the time goes in v1:
time: 261 us; the launch traced here: 260 us
  other arithmetic  127 us (49%)
  Pallas kernels  42 us (16%)
  local copies, waits for them, and re-layouts  34.6 us (13%)
  matrix products  29 us (11%)
  starting transfers between devices  22 us (8%)
  waiting for transfers between devices  3.21 us (1%)
    reduce_sum x8, other arithmetic, partials(): tap_sums.append(jnp.sum(shifted * d_conv, axis=(0, 1)))  42.4 us
    pallas_call x1, Pallas kernels, reduce_all(): pl.pallas_call(functools.partial(reduce_kernel, factor), out_shape=(jax.S...  42 us
    convert_element_type x1, other arithmetic, body(): grad_image = (cotangent.astype(jnp.float32) + transposed(d_padded, conv_k...  36.7 us
    reduce_sum x1, other arithmetic, layer_pass(): average = jnp.mean(conv_out, axis=-1, keepdims=True)  34.9 us
    ppermute x4, starting transfers between devices, padded_2(): before = lax.ppermute(last, axis, up)  14.6 us
    ppermute x4, starting transfers between devices, padded_2(): after = lax.ppermute(first, axis, down)  7.46 us
    dot_general x1, matrix products, layer_pass(): lax.dot_general(scaled, out_weight, (((1,), (1,)), ((), ())), preferred_e...  6.05 us
    dot_general x1, matrix products, layer_pass(): jnp.dot(activation, out_weight, preferred_element_type=jnp.float32)  5.83 us
  transfers between devices with their start and end apart: 8, of which 1 were waited for; matrix products, arithmetic and copies ran while one was open for 21% of the time, Pallas kernels for 16%

profile of v1, /device:TPU:1, one launch (start us, length us, event | category | flops | bytes accessed | tf_op | source)
XLA Modules:
  0.0 259.8 jit_solution(17458057010169420998)
XLA Ops:
  1.9 4.0 %collective-permute-start = (bf16[3,192,192]{2,1,0:T(8,128)(2,1)S(1)}, bf16[3,192,192]{2,1,0:T(8,128)(2,1)S(1)}, u32[]{:S(2)}, u32[]{:S(2)}) collective-permute-start(bf16[3,192,192]{2,1,0:T(8,128)(2,1)S(1)} %get-tuple-element.105), channel_id=1, source_target_pairs={{0,8},{8,16},{16,24},{24,32},{32,40},{40,48},{48,56},{56,64},{64,7... | collective-permute-start | bytes 663560 | tf_op jit(solution)/shard_map/ppermute | solution.py:19
  12.2 3.2 %collective-permute-done.1 = bf16[3,192,192]{2,1,0:T(8,128)(2,1)S(1)} collective-permute-done((bf16[3,192,192]{2,1,0:T(8,128)(2,1)S(1)}, bf16[3,192,192]{2,1,0:T(8,128)(2,1)S(1)}, u32[]{:S(2)}, u32[]{:S(2)}) %collective-permute-start.1) | collective-permute-done | bytes 221216 | tf_op jit(solution)/shard_map/ppermute | solution.py:20
  16.7 4.9 %collective-permute-start.2 = (bf16[22,3,192]{2,1,0:T(4,128)(2,1)S(1)}, bf16[22,3,192]{2,1,0:T(4,128)(2,1)S(1)}, u32[]{:S(2)}, u32[]{:S(2)}) collective-permute-start(bf16[22,3,192]{2,1,0:T(4,128)(2,1)S(1)} %get-tuple-element.97), channel_id=1, source_target_pairs={{0,1},{1,2},{2,3},{3,4},{4,5},{5,6},{6,7},{8,9},{9,10},{10,11},{11... | collective-permute-start | bytes 76040 | tf_op jit(solution)/shard_map/ppermute | solution.py:19
  21.6 1.9 collective-permute-start.3
  24.0 2.9 %copy.33 = f32[3072,192]{0,1:T(8,128)} copy(bf16[3072,192]{1,0:T(8,128)(2,1)} %bitcast.134) | data formatting | bytes 3538944 | tf_op jit(solution)/shard_map/reshape | solution.py:84
  26.9 2.8 %copy.31 = f32[3072,192]{0,1:T(8,128)} copy(bf16[3072,192]{1,0:T(8,128)(2,1)} %bitcast.129) | data formatting | bytes 3538944 | tf_op jit(solution)/shard_map/reshape | solution.py:82
  30.6 34.9 %fusion.152 = (f32[16,192]{1,0:T(8,128)S(1)}, f32[16,192,192]{2,1,0:T(8,128)S(1)}) fusion(f32[192]{0:T(256)S(1)} %copy-done.105, f32[192]{0:T(256)} %bitcast.49, bf16[22,3,192]{2,1,0:T(4,128)(2,1)S(1)} %collective-permute-done.3, bf16[22,192,192]{2,1,0:T(8,128)(2,1)S(1)} %get-tuple-element.109, f32[192]{0:T(256)} %bitcast.48, f32[192]{0:T(256)S(1)} %bitcast.138, ...), kind=kLoop, calls=%fused_computation.335 | loop fusion | flops 161608704 | bytes 12340224 | tf_op jit(solution)/shard_map/reduce_sum | solution.py:70
  68.5 2.4 copy.35
  70.9 5.4 %multiply_convert_fusion = (bf16[3072,768]{1,0:T(8,128)(2,1)}, f32[3072,768]{1,0:T(8,128)S(1)}) fusion(f32[768]{0:T(1024)S(1)} %copy-done.26, bf16[3072,192]{1,0:T(8,128)(2,1)} %bitcast.132, bf16[192,768]{1,0:T(8,128)(2,1)S(1)} %copy-done), kind=kOutput, calls=%fused_computation.46 | convolution fusion | flops 920125440 | bytes 15633408 | tf_op jit(solution)/shard_map/dot_general | solution.py:76
  76.4 6.1 %fusion.162 = (f32[768]{0:T(1024)}, bf16[3072,768]{1,0:T(8,128)(2,1)S(1)}) fusion(f32[3072,768]{1,0:T(8,128)S(1)} %get-tuple-element.168, f32[768]{0:T(1024)S(1)} %copy-done.26, bf16[768,192]{0,1:T(8,128)(2,1)S(1)} %copy-done.22, f32[3072,192]{0,1:T(8,128)S(1)} %copy-done.14, f32[192]{0:T(256)S(1)} %copy-done.28), kind=kOutput, calls=%fused_computation.344 | convolution fusion | flops 935460096 | bytes 16816896 | tf_op jit(solution)/shard_map/dot_general | solution.py:86
  82.4 2.3 fusion.102
  84.7 3.7 %fusion.151 = (f32[192]{0:T(256)S(1)}, f32[192]{0:T(256)}, f32[3072]{0:T(1024)}, f32[3072,192]{0,1:T(8,128)}) fusion(f32[3072,192]{0,1:T(8,128)S(1)} %copy-done.19, f32[192]{0:T(256)S(1)} %copy-done.25, bf16[192,768]{1,0:T(8,128)(2,1)S(1)} %copy-done, bf16[3072,768]{1,0:T(8,128)(2,1)S(1)} %get-tuple-element.170), kind=kOutput, calls=%fused_computation.334 | convolution fusion | flops 908915328 | bytes 9746688 | tf_op jit(solution)/shard_map/dot_general | solution.py:91
  88.5 3.5 %copy.34 = f32[3072,192]{1,0:T(8,128)} copy(f32[3072,192]{0,1:T(8,128)} %get-tuple-element.166) | data formatting | bytes 4718592 | tf_op jit(solution)/shard_map/reshape | solution.py:94
  91.9 2.5 multiply_reduce_fusion.1
  94.6 12.2 %fusion.100 = (f32[192]{0:T(256)}, f32[192]{0:T(256)}, f32[192]{0:T(256)}, f32[192]{0:T(256)}, f32[192]{0:T(256)}, /*index=5*/f32[192]{0:T(256)}, f32[192]{0:T(256)}, f32[16,192,192]{2,1,0:T(8,128)S(1)}) fusion(bf16[22,3,192]{2,1,0:T(4,128)(2,1)S(1)} %collective-permute-done.3, bf16[22,192,192]{2,1,0:T(8,128)(2,1)} %copy-done.2, ...), kind=kLoop, calls=%fused_computation.240 | loop fusion | flops 24771264 | bytes 8768256 | tf_op jit(solution)/shard_map/reduce_sum | solution.py:143
  106.8 3.3 %fusion.97 = (f32[192]{0:T(256)S(1)}, f32[192]{0:T(256)S(1)}, f32[192]{0:T(256)S(1)}, f32[192]{0:T(256)}, f32[192]{0:T(256)}, /*index=5*/f32[192]{0:T(256)}, f32[192]{0:T(256)}) fusion(f32[16,192,192]{2,1,0:T(8,128)S(1)} %get-tuple-element.85, bf16[19,192,192]{2,1,0:T(8,128)(2,1)S(1)} %copy-done.5, bf16[16,192,192]{2,1,0:T(8,128)(2,1)S(1)} %copy-done.10, ...), kind=kLoop, calls=%fused_computation.237 | loop fusion | flops 12384960 | bytes 10622208 | tf_op jit(solution)/shard_map/reduce_sum | solution.py:143
  110.2 5.6 %fusion.150 = f32[768,192]{1,0:T(8,128)} fusion(bf16[3072,768]{1,0:T(8,128)(2,1)} %get-tuple-element.167, f32[3072,192]{0,1:T(8,128)} %copy.33, f32[192]{0:T(256)S(1)} %copy-done.29), kind=kOutput, calls=%fused_computation.333 | convolution fusion | flops 907149312 | bytes 7668480 | tf_op jit(solution)/shard_map/dot_general | solution.py:155
  115.8 4.4 %fusion.96 = (f32[192]{0:T(256)}, f32[192]{0:T(256)}, f32[192]{0:T(256)}, f32[192]{0:T(256)}, f32[192]{0:T(256)}, /*index=5*/f32[192]{0:T(256)}, bf16[16,192,192]{2,1,0:T(8,128)(2,1)S(1)}) fusion(f32[16,192,192]{2,1,0:T(8,128)S(1)} %get-tuple-element.85, bf16[22,192,192]{2,1,0:T(8,128)(2,1)S(1)} %copy-done.3, bf16[22,3,192]{2,1,0:T(4,128)(2,1)S(1)} %collective-permute-done.2), kind=kLoop, calls=%fused_computation.236 | loop fusion | flops 21822336 | bytes 5190912 | tf_op jit(solution)/shard_map/reduce_sum | solution.py:143
  122.2 3.1 %collective-permute-start.4 = (bf16[3,192,192]{2,1,0:T(8,128)(2,1)}, bf16[3,192,192]{2,1,0:T(8,128)(2,1)S(1)}, u32[]{:S(2)}, u32[]{:S(2)}) collective-permute-start(bf16[3,192,192]{2,1,0:T(8,128)(2,1)} %get-tuple-element.100), channel_id=1, source_target_pairs={{0,8},{8,16},{16,24},{24,32},{32,40},{40,48},{48,56},{56,64},{64,7... | collective-permute-start | bytes 663560 | tf_op jit(solution)/shard_map/ppermute | solution.py:19
  126.6 5.8 %multiply_reduce_fusion.3 = (f32[192]{0:T(256)}, bf16[3072,192]{0,1:T(8,128)(2,1)}) fusion(f32[3072,192]{0,1:T(8,128)S(1)} %copy-done.15, f32[3072,192]{0,1:T(8,128)S(1)} %copy-done.16, f32[192]{0:T(256)S(1)} %copy-done.29, f32[192]{0:T(256)S(1)} %copy-done.102, bf16[3072,768]{1,0:T(8,128)(2,1)} %get-tuple-element.167, bf16[768,192]{0,1:T(8,128)(2,1)S(1)} %copy-done.23), kind=kOutput, calls=%fused_computation.253 | convolution fusion | flops 909508416 | bytes 10914048 | tf_op jit(solution)/shard_map/dot_general | solution.py:81
  132.5 4.8 %fusion.86 = (f32[192]{0:T(256)}, f32[192]{0:T(256)}, f32[192]{0:T(256)}, f32[192]{0:T(256)}, f32[192]{0:T(256)}, /*index=5*/f32[192]{0:T(256)}) fusion(f32[16,192,192]{2,1,0:T(8,128)S(1)} %get-tuple-element.85, bf16[22,3,192]{2,1,0:T(4,128)(2,1)S(1)} %collective-permute-done.3, bf16[22,192,192]{2,1,0:T(8,128)(2,1)S(1)} %copy-done.3), kind=kLoop, calls=%fused_computation.226 | loop fusion | flops 21232512 | bytes 4011264 | tf_op jit(solution)/shard_map/reduce_sum | solution.py:143
  137.3 4.2 %fusion.82 = (f32[192]{0:T(256)}, f32[192]{0:T(256)}, f32[192]{0:T(256)}, f32[192]{0:T(256)}, f32[192]{0:T(256)}, /*index=5*/f32[192]{0:T(256)}) fusion(f32[16,192,192]{2,1,0:T(8,128)S(1)} %get-tuple-element.85, bf16[22,3,192]{2,1,0:T(4,128)(2,1)S(1)} %collective-permute-done.2, bf16[22,192,192]{2,1,0:T(8,128)(2,1)S(1)} %copy-done.3), kind=kLoop, calls=%fused_computation.222 | loop fusion | flops 21232512 | bytes 4011264 | tf_op jit(solution)/shard_map/reduce_sum | solution.py:143
  141.5 4.8 %fusion.50 = (f32[192]{0:T(256)}, f32[192]{0:T(256)}, f32[192]{0:T(256)}, f32[192]{0:T(256)}, f32[192]{0:T(256)}, /*index=5*/f32[192]{0:T(256)}) fusion(f32[16,192,192]{2,1,0:T(8,128)S(1)} %get-tuple-element.85, bf16[22,3,192]{2,1,0:T(4,128)(2,1)S(1)} %collective-permute-done.3, bf16[22,192,192]{2,1,0:T(8,128)(2,1)S(1)} %copy-done.3), kind=kLoop, calls=%fused_computation.190 | loop fusion | flops 21232512 | bytes 4011264 | tf_op jit(solution)/shard_map/reduce_sum | solution.py:143
  146.3 4.2 %fusion.46 = (f32[192]{0:T(256)}, f32[192]{0:T(256)}, f32[192]{0:T(256)}, f32[192]{0:T(256)}, f32[192]{0:T(256)}, /*index=5*/f32[192]{0:T(256)}) fusion(f32[16,192,192]{2,1,0:T(8,128)S(1)} %get-tuple-element.85, bf16[22,3,192]{2,1,0:T(4,128)(2,1)S(1)} %collective-permute-done.2, bf16[22,192,192]{2,1,0:T(8,128)(2,1)S(1)} %copy-done.3), kind=kLoop, calls=%fused_computation.186 | loop fusion | flops 21232512 | bytes 4011264 | tf_op jit(solution)/shard_map/reduce_sum | solution.py:143
  150.5 4.5 %fusion.36 = (f32[192]{0:T(256)}, f32[192]{0:T(256)}, f32[192]{0:T(256)}, f32[192]{0:T(256)}, f32[192]{0:T(256)}, /*index=5*/f32[192]{0:T(256)}) fusion(f32[16,192,192]{2,1,0:T(8,128)S(1)} %get-tuple-element.85, bf16[22,3,192]{2,1,0:T(4,128)(2,1)S(1)} %collective-permute-done.3, bf16[22,192,192]{2,1,0:T(8,128)(2,1)S(1)} %copy-done.3, ...), kind=kLoop, calls=%fused_computation.176 | loop fusion | flops 21232512 | bytes 4036608 | tf_op jit(solution)/shard_map/reduce_sum | solution.py:143
  155.1 5.3 %concatenate.137 = f32[58,192]{1,0:T(8,128)S(1)} concatenate(f32[1,192]{1,0:T(1,128)} %bitcast.252, f32[1,192]{1,0:T(1,128)} %bitcast.253, f32[1,192]{1,0:T(1,128)} %bitcast.254, f32[1,192]{1,0:T(1,128)} %bitcast.214, f32[1,192]{1,0:T(1,128)} %bitcast.251, f32[1,192]{1,0:T(1,128)} %bitcast.250, f32[1,192]{1,0:T(1,128)} %bitcast.249, f32[1,192]{1,0:T(1,128)} %bitcast.247, ...), dimensions={0} | concatenate | bytes 89088 | tf_op jit(solution)/shard_map/concatenate | solution.py:504
  161.0 2.7 %pad_maximum_fusion.5.w_ref = f32[768,384]{1,0:T(8,128)} fusion(f32[768,192]{1,0:T(8,128)} %fusion.150, f32[768,192]{1,0:T(8,128)} %fusion.102), kind=kLoop, calls=%fused_computation.317 | loop fusion | flops 294912 | bytes 2359296 | tf_op jit(solution)/shard_map/concatenate | solution.py:503
  163.8 42.0 %shard_map.194 = (f32[24,384]{1,0:T(8,128)}, f32[64,256]{1,0:T(8,128)}) custom-call(f32[768,384]{1,0:T(8,128)} %pad_maximum_fusion.5.w_ref, f32[64,256]{1,0:T(8,128)} %pad.4.s_ref), custom_call_target="tpu_custom_call" | custom-call | tf_op jit(solution)/shard_map/pallas_call | solution.py:423
  208.1 3.0 %collective-permute-start.6 = (bf16[22,3,192]{2,1,0:T(4,128)(2,1)S(1)}, bf16[22,3,192]{2,1,0:T(4,128)(2,1)S(1)}, u32[]{:S(2)}, u32[]{:S(2)}) collective-permute-start(bf16[22,3,192]{2,1,0:T(4,128)(2,1)S(1)} %get-tuple-element.95), channel_id=1, source_target_pairs={{1,0},{2,1},{3,2},{4,3},{5,4},{6,5},{7,6},{9,8},{10,9},{11,10},{12... | collective-permute-start | bytes 76040 | tf_op jit(solution)/shard_map/ppermute | solution.py:20
  211.1 2.6 %collective-permute-start.7 = (bf16[22,3,192]{2,1,0:T(4,128)(2,1)S(1)}, bf16[22,3,192]{2,1,0:T(4,128)(2,1)S(1)}, u32[]{:S(2)}, u32[]{:S(2)}) collective-permute-start(bf16[22,3,192]{2,1,0:T(4,128)(2,1)S(1)} %get-tuple-element.96), channel_id=1, source_target_pairs={{0,1},{1,2},{2,3},{3,4},{4,5},{5,6},{6,7},{8,9},{9,10},{10,11},{11... | collective-permute-start | bytes 76040 | tf_op jit(solution)/shard_map/ppermute | solution.py:19
  219.9 2.6 %pad_maximum_fusion = (bf16[22,195,192]{2,1,0:T(8,128)(2,1)S(1)}, bf16[22,195,192]{2,1,0:T(8,128)(2,1)S(1)}) fusion(bf16[22,3,192]{2,1,0:T(4,128)(2,1)S(1)} %collective-permute-done.6, bf16[3,192,192]{2,1,0:T(8,128)(2,1)} %collective-permute-done.5, bf16[16,192,192]{2,1,0:T(8,128)(2,1)S(1)} %copy-done.12, ...), kind=kLoop, calls=%fused_computation.262 | loop fusion | flops 13178880 | bytes 4967424 | tf_op jit(solution)/shard_map/concatenate | solution.py:21
  222.9 36.7 %add_convert_fusion = bf16[16,192,192]{2,1,0:T(8,128)(2,1)} fusion(bf16[16,192,192]{2,1,0:T(8,128)(2,1)S(1)} %copy-done.12, bf16[3,192,192]{2,1,0:T(8,128)(2,1)} %copy-done.21, bf16[3,192,192]{2,1,0:T(8,128)(2,1)} %collective-permute-done.5, bf16[22,195,192]{2,1,0:T(8,128)(2,1)S(1)} %get-tuple-element.94, bf16[22,195,192]{2,1,0:T(8,128)(2,1)S(1)} %get-tuple-element.93, ...), kind=kLoop, calls=%fused_computation.242 | loop fusion | flops 91422720 | bytes 53564160 | tf_op jit(solution)/shard_map/convert_element_type | solution.py:489
  (252 shorter events, 25.1 us)
Async XLA Ops:
  0.6 70.2 %copy-start = (bf16[192,768]{1,0:T(8,128)(2,1)S(1)}, bf16[192,768]{1,0:T(8,128)(2,1)}, u32[]{:S(2)}) copy-start(bf16[192,768]{1,0:T(8,128)(2,1)} %param.16) | copy-start | bytes 884740
  1.9 9.8 %collective-permute-start = (bf16[3,192,192]{2,1,0:T(8,128)(2,1)S(1)}, bf16[3,192,192]{2,1,0:T(8,128)(2,1)S(1)}, u32[]{:S(2)}, u32[]{:S(2)}) collective-permute-start(bf16[3,192,192]{2,1,0:T(8,128)(2,1)S(1)} %get-tuple-element.105), channel_id=1, source_target_pairs={{0,8},{8,16},{16,24},{24,32},{32,40},{40,48},{48,56},{56,64},{64,7... | collective-permute-start | bytes 663560 | tf_op jit(solution)/shard_map/ppermute | solution.py:19
  5.9 9.5 %collective-permute-start.1 = (bf16[3,192,192]{2,1,0:T(8,128)(2,1)S(1)}, bf16[3,192,192]{2,1,0:T(8,128)(2,1)S(1)}, u32[]{:S(2)}, u32[]{:S(2)}) collective-permute-start(bf16[3,192,192]{2,1,0:T(8,128)(2,1)S(1)} %get-tuple-element.104), channel_id=1, source_target_pairs={{8,0},{16,8},{24,16},{32,24},{40,32},{48,40},{56,48},{64,56},{72,6... | collective-permute-start | bytes 663560 | tf_op jit(solution)/shard_map/ppermute | solution.py:20
  8.2 22.1 %copy-start.30 = (f32[1,1,192]{2,1,0:T(1,128)}, f32[1,1,192]{2,1,0:T(1,128)S(1)}, u32[]{:S(2)}) copy-start(f32[1,1,192]{2,1,0:T(1,128)S(1)} %get-tuple-element.115) | copy-start | bytes 2308
  8.2 22.1 %copy-start.32 = (f32[1,1,192]{2,1,0:T(1,128)}, f32[1,1,192]{2,1,0:T(1,128)S(1)}, u32[]{:S(2)}) copy-start(f32[1,1,192]{2,1,0:T(1,128)S(1)} %get-tuple-element.116) | copy-start | bytes 2308
  8.2 22.1 %copy-start.34 = (f32[1,1,192]{2,1,0:T(1,128)}, f32[1,1,192]{2,1,0:T(1,128)S(1)}, u32[]{:S(2)}) copy-start(f32[1,1,192]{2,1,0:T(1,128)S(1)} %get-tuple-element.117) | copy-start | bytes 2308
  8.2 22.1 %copy-start.36 = (f32[1,1,192]{2,1,0:T(1,128)}, f32[1,1,192]{2,1,0:T(1,128)S(1)}, u32[]{:S(2)}) copy-start(f32[1,1,192]{2,1,0:T(1,128)S(1)} %get-tuple-element.118) | copy-start | bytes 2308
  8.2 22.1 %copy-start.38 = (f32[1,1,192]{2,1,0:T(1,128)}, f32[1,1,192]{2,1,0:T(1,128)S(1)}, u32[]{:S(2)}) copy-start(f32[1,1,192]{2,1,0:T(1,128)S(1)} %get-tuple-element.119) | copy-start | bytes 2308
  8.2 22.1 %copy-start.40 = (f32[1,1,192]{2,1,0:T(1,128)}, f32[1,1,192]{2,1,0:T(1,128)S(1)}, u32[]{:S(2)}) copy-start(f32[1,1,192]{2,1,0:T(1,128)S(1)} %get-tuple-element.120) | copy-start | bytes 2308
  8.2 22.1 %copy-start.42 = (f32[1,1,192]{2,1,0:T(1,128)}, f32[1,1,192]{2,1,0:T(1,128)S(1)}, u32[]{:S(2)}) copy-start(f32[1,1,192]{2,1,0:T(1,128)S(1)} %get-tuple-element.121) | copy-start | bytes 2308
  8.2 22.1 %copy-start.44 = (f32[1,1,192]{2,1,0:T(1,128)}, f32[1,1,192]{2,1,0:T(1,128)S(1)}, u32[]{:S(2)}) copy-start(f32[1,1,192]{2,1,0:T(1,128)S(1)} %get-tuple-element.122) | copy-start | bytes 2308
  8.2 22.1 %copy-start.46 = (f32[1,1,192]{2,1,0:T(1,128)}, f32[1,1,192]{2,1,0:T(1,128)S(1)}, u32[]{:S(2)}) copy-start(f32[1,1,192]{2,1,0:T(1,128)S(1)} %get-tuple-element.123) | copy-start | bytes 2308
  8.2 22.1 %copy-start.48 = (f32[1,1,192]{2,1,0:T(1,128)}, f32[1,1,192]{2,1,0:T(1,128)S(1)}, u32[]{:S(2)}) copy-start(f32[1,1,192]{2,1,0:T(1,128)S(1)} %get-tuple-element.124) | copy-start | bytes 2308
  8.3 22.1 %copy-start.50 = (f32[1,1,192]{2,1,0:T(1,128)}, f32[1,1,192]{2,1,0:T(1,128)S(1)}, u32[]{:S(2)}) copy-start(f32[1,1,192]{2,1,0:T(1,128)S(1)} %get-tuple-element.125) | copy-start | bytes 2308
  8.3 22.1 %copy-start.52 = (f32[1,1,192]{2,1,0:T(1,128)}, f32[1,1,192]{2,1,0:T(1,128)S(1)}, u32[]{:S(2)}) copy-start(f32[1,1,192]{2,1,0:T(1,128)S(1)} %get-tuple-element.126) | copy-start | bytes 2308
  8.3 22.1 %copy-start.54 = (f32[1,1,192]{2,1,0:T(1,128)}, f32[1,1,192]{2,1,0:T(1,128)S(1)}, u32[]{:S(2)}) copy-start(f32[1,1,192]{2,1,0:T(1,128)S(1)} %get-tuple-element.127) | copy-start | bytes 2308
  8.3 22.1 %copy-start.56 = (f32[1,1,192]{2,1,0:T(1,128)}, f32[1,1,192]{2,1,0:T(1,128)S(1)}, u32[]{:S(2)}) copy-start(f32[1,1,192]{2,1,0:T(1,128)S(1)} %get-tuple-element.128) | copy-start | bytes 2308
  8.3 22.1 %copy-start.58 = (f32[1,1,192]{2,1,0:T(1,128)}, f32[1,1,192]{2,1,0:T(1,128)S(1)}, u32[]{:S(2)}) copy-start(f32[1,1,192]{2,1,0:T(1,128)S(1)} %get-tuple-element.129) | copy-start | bytes 2308
  8.3 22.1 %copy-start.60 = (f32[1,1,192]{2,1,0:T(1,128)}, f32[1,1,192]{2,1,0:T(1,128)S(1)}, u32[]{:S(2)}) copy-start(f32[1,1,192]{2,1,0:T(1,128)S(1)} %get-tuple-element.130) | copy-start | bytes 2308
  8.3 22.1 %copy-start.62 = (f32[1,1,192]{2,1,0:T(1,128)}, f32[1,1,192]{2,1,0:T(1,128)S(1)}, u32[]{:S(2)}) copy-start(f32[1,1,192]{2,1,0:T(1,128)S(1)} %get-tuple-element.131) | copy-start | bytes 2308
  8.3 22.1 %copy-start.64 = (f32[1,1,192]{2,1,0:T(1,128)}, f32[1,1,192]{2,1,0:T(1,128)S(1)}, u32[]{:S(2)}) copy-start(f32[1,1,192]{2,1,0:T(1,128)S(1)} %get-tuple-element.132) | copy-start | bytes 2308
  8.3 22.1 %copy-start.66 = (f32[1,1,192]{2,1,0:T(1,128)}, f32[1,1,192]{2,1,0:T(1,128)S(1)}, u32[]{:S(2)}) copy-start(f32[1,1,192]{2,1,0:T(1,128)S(1)} %get-tuple-element.133) | copy-start | bytes 2308
  16.7 13.5 %collective-permute-start.2 = (bf16[22,3,192]{2,1,0:T(4,128)(2,1)S(1)}, bf16[22,3,192]{2,1,0:T(4,128)(2,1)S(1)}, u32[]{:S(2)}, u32[]{:S(2)}) collective-permute-start(bf16[22,3,192]{2,1,0:T(4,128)(2,1)S(1)} %get-tuple-element.97), channel_id=1, source_target_pairs={{0,1},{1,2},{2,3},{3,4},{4,5},{5,6},{6,7},{8,9},{9,10},{10,11},{11... | collective-permute-start | bytes 76040 | tf_op jit(solution)/shard_map/ppermute | solution.py:19
  21.6 8.6 %collective-permute-start.3 = (bf16[22,3,192]{2,1,0:T(4,128)(2,1)S(1)}, bf16[22,3,192]{2,1,0:T(4,128)(2,1)S(1)}, u32[]{:S(2)}, u32[]{:S(2)}) collective-permute-start(bf16[22,3,192]{2,1,0:T(4,128)(2,1)S(1)} %get-tuple-element.98), channel_id=1, source_target_pairs={{1,0},{2,1},{3,2},{4,3},{5,4},{6,5},{7,6},{9,8},{10,9},{11,10},{12... | collective-permute-start | bytes 76040 | tf_op jit(solution)/shard_map/ppermute | solution.py:20
  68.5 23.5 %copy-start.8 = (f32[16,192,192]{2,1,0:T(8,128)}, f32[16,192,192]{2,1,0:T(8,128)S(1)}, u32[]{:S(2)}) copy-start(f32[16,192,192]{2,1,0:T(8,128)S(1)} %get-tuple-element.87) | copy-start | bytes 7077892
  122.2 85.1 %collective-permute-start.4 = (bf16[3,192,192]{2,1,0:T(8,128)(2,1)}, bf16[3,192,192]{2,1,0:T(8,128)(2,1)S(1)}, u32[]{:S(2)}, u32[]{:S(2)}) collective-permute-start(bf16[3,192,192]{2,1,0:T(8,128)(2,1)} %get-tuple-element.100), channel_id=1, source_target_pairs={{0,8},{8,16},{16,24},{24,32},{32,40},{40,48},{48,56},{56,64},{64,7... | collective-permute-start | bytes 663560 | tf_op jit(solution)/shard_map/ppermute | solution.py:19
  125.3 82.0 %collective-permute-start.5 = (bf16[3,192,192]{2,1,0:T(8,128)(2,1)}, bf16[3,192,192]{2,1,0:T(8,128)(2,1)}, u32[]{:S(2)}, u32[]{:S(2)}) collective-permute-start(bf16[3,192,192]{2,1,0:T(8,128)(2,1)} %get-tuple-element.99), channel_id=1, source_target_pairs={{8,0},{16,8},{24,16},{32,24},{40,32},{48,40},{56,48},{64,56},{72,6... | collective-permute-start | bytes 663560 | tf_op jit(solution)/shard_map/ppermute | solution.py:20
  155.1 52.2 %copy-start.12 = (bf16[16,192,192]{2,1,0:T(8,128)(2,1)S(1)}, bf16[16,192,192]{2,1,0:T(8,128)(2,1)}, u32[]{:S(2)}) copy-start(bf16[16,192,192]{2,1,0:T(8,128)(2,1)} %copy-done.11) | copy-start | bytes 3538948
  161.0 56.4 %copy-start.20 = (bf16[3072,192]{0,1:T(8,128)(2,1)S(1)}, bf16[3072,192]{0,1:T(8,128)(2,1)}, u32[]{:S(2)}) copy-start(bf16[3072,192]{0,1:T(8,128)(2,1)} %get-tuple-element.92) | copy-start | bytes 3538948
  208.1 11.8 %collective-permute-start.6 = (bf16[22,3,192]{2,1,0:T(4,128)(2,1)S(1)}, bf16[22,3,192]{2,1,0:T(4,128)(2,1)S(1)}, u32[]{:S(2)}, u32[]{:S(2)}) collective-permute-start(bf16[22,3,192]{2,1,0:T(4,128)(2,1)S(1)} %get-tuple-element.95), channel_id=1, source_target_pairs={{1,0},{2,1},{3,2},{4,3},{5,4},{6,5},{7,6},{9,8},{10,9},{11,10},{12... | collective-permute-start | bytes 76040 | tf_op jit(solution)/shard_map/ppermute | solution.py:20
  211.1 8.8 %collective-permute-start.7 = (bf16[22,3,192]{2,1,0:T(4,128)(2,1)S(1)}, bf16[22,3,192]{2,1,0:T(4,128)(2,1)S(1)}, u32[]{:S(2)}, u32[]{:S(2)}) collective-permute-start(bf16[22,3,192]{2,1,0:T(4,128)(2,1)S(1)} %get-tuple-element.96), channel_id=1, source_target_pairs={{0,1},{1,2},{2,3},{3,4},{4,5},{5,6},{6,7},{8,9},{9,10},{10,11},{11... | collective-permute-start | bytes 76040 | tf_op jit(solution)/shard_map/ppermute | solution.py:19
  222.9 36.7 %copy-start.1 = (bf16[192,768]{1,0:T(8,128)(2,1)S(1)}, bf16[192,768]{1,0:T(8,128)(2,1)}, u32[]{:S(2)}) copy-start(bf16[192,768]{1,0:T(8,128)(2,1)} %param.16) | copy-start | bytes 884740
  (83 other events, 660.4 us)

commit v2 on v1

--- a/solution.py
+++ b/solution.py
@@ -28,149 +28,255 @@
     return (hidden * normal_cdf, normal_cdf + hidden * normal_pdf)
 
 
-def depthwise(padded, conv_kernel, n_rows, n_cols):
-    accum = jnp.zeros((n_rows, n_cols, conv_kernel.shape[2]), jnp.float32)
-    for row_tap in range(7):
-        for col_tap in range(7):
-            shifted = padded[row_tap : row_tap + n_rows, col_tap : col_tap + n_cols].astype(
-                jnp.float32
-            )
-            accum = accum + shifted * conv_kernel[row_tap, col_tap]
+def widen(source_ref, main_ref, rest_ref):
+    n_rows, n_cols, _ = source_ref.shape
+
+    def step(i, carry):
+        row = source_ref[i].astype(jnp.float32)
+        row = jnp.concatenate([row, jnp.zeros((200 - n_cols, 192), jnp.float32)], axis=0)
+        main_ref[i] = row[:, 0:128]
+        rest_ref[i] = jnp.concatenate([row[0:104, 128:192], row[96:200, 128:192]], axis=1)
+        return carry
+
+    lax.fori_loop(0, n_rows, step, 0)
+
+
+def tile_of(wide_ref, taps_ref, first, start, flip):
+    n_rows = wide_ref.shape[0] - 6
+    accum = jnp.zeros((n_rows, 8, 128), jnp.float32)
+    for b in range(7):
+        shifted = wide_ref[:, pl.ds(start + b, 8), :]
+        for a in range(7):
+            tap = 48 - (7 * a + b) if flip else 7 * a + b
+            accum = accum + shifted[a : a + n_rows] * taps_ref[tap, first : first + 128]
     return accum
 
 
-def transposed(d_padded, conv_kernel, n_rows, n_cols):
-    accum = jnp.zeros((n_rows, n_cols, conv_kernel.shape[2]), jnp.float32)
-    for row_tap in range(7):
-        for col_tap in range(7):
-            shifted = d_padded[
-                6 - row_tap : 6 - row_tap + n_rows, 6 - col_tap : 6 - col_tap + n_cols
-            ].astype(jnp.float32)
-            accum = accum + shifted * conv_kernel[row_tap, col_tap]
-    return accum
-
-
-def layer_pass(
-    padded,
-    cotangent,
-    conv_kernel,
-    conv_bias,
-    norm_gain,
-    norm_bias,
-    in_weight,
-    in_bias,
-    out_weight,
-    out_bias,
-    layer_scale,
+def convolve(main_ref, rest_ref, taps_ref, flip, out_ref):
+    def main_step(i, carry):
+        start = pl.multiple_of(8 * i, 8)
+        out_ref[:, pl.ds(start, 8), 0:128] = tile_of(main_ref, taps_ref, 0, start, flip)
+        return carry
+
+    def rest_step(i, carry):
+        start = pl.multiple_of(8 * i, 8)
+        tile = tile_of(rest_ref, taps_ref, 128, start, flip)
+        out_ref[:, pl.ds(start, 8), 128:192] = tile[:, :, 0:64]
+        out_ref[:, pl.ds(start + 96, 8), 128:192] = tile[:, :, 64:128]
+        return carry
+
+    lax.fori_loop(0, 24, main_step, 0)
+    lax.fori_loop(0, 12, rest_step, 0)
+
+
+def tap_sums(main_ref, rest_ref, d_main_ref, d_rest_ref, sums_ref):
+    n_rows = d_main_ref.shape[0]
+    for wide_ref, d_ref, first, steps in (
+        (main_ref, d_main_ref, 0, 24),
+        (rest_ref, d_rest_ref, 128, 12),
+    ):
+
+        def step(i, carry, wide_ref=wide_ref, d_ref=d_ref, first=first):
+            start = pl.multiple_of(8 * i, 8)
+            d_tile = d_ref[:, pl.ds(start, 8), :]
+            for b in range(7):
+                shifted = wide_ref[:, pl.ds(start + b, 8), :]
+                for a in range(7):
+                    tap = 7 * a + b
+                    sums_ref[tap, :, first : first + 128] += jnp.sum(
+                        shifted[a : a + n_rows] * d_tile, axis=0
+                    )
+            return carry
+
+        lax.fori_loop(0, steps, step, 0)
+
+
+def fold(values):
+    return jnp.sum(values.reshape(values.shape[0] // 8, 8, values.shape[1]), axis=0)
+
+
+CHUNK = 2
+
+
+def block_kernel(
+    padded_ref,
+    image_ref,
+    cot_ref,
+    taps_ref,
+    rows_ref,
+    in_weight_ref,
+    in_weight_t_ref,
+    in_bias_ref,
+    out_weight_ref,
+    out_weight_t_ref,
+    output_ref,
+    d_conv_ref,
+    w_ref,
+    s_ref,
+    main_ref,
+    rest_ref,
+    conv_ref,
+    d_main_ref,
+    d_rest_ref,
+    sums_ref,
+    tap_ref,
+    bias_sum_ref,
+    g_in_ref,
+    g_out_ref,
 ):
+    n_rows, n_cols, channels = image_ref.shape
+    pixels = CHUNK * n_cols
+    widen(padded_ref, main_ref, rest_ref)
+    sums_ref[...] = jnp.zeros_like(sums_ref)
+    tap_ref[...] = jnp.zeros_like(tap_ref)
+    bias_sum_ref[...] = jnp.zeros_like(bias_sum_ref)
+    g_in_ref[...] = jnp.zeros_like(g_in_ref)
+    g_out_ref[...] = jnp.zeros_like(g_out_ref)
+
+    convolve(main_ref, rest_ref, taps_ref, False, conv_ref)
+
+    def chunk(i, carry):
+        span = pl.ds(CHUNK * i, CHUNK)
+        conv_bias, gain, norm_bias = rows_ref[0:1], rows_ref[1:2], rows_ref[2:3]
+        out_bias, layer_scale = rows_ref[3:4], rows_ref[4:5]
+        conv_out = conv_ref[span].reshape(pixels, channels) + conv_bias
+        centred = conv_out - jnp.mean(conv_out, axis=-1, keepdims=True)
+        inv_std = lax.rsqrt(jnp.mean(centred * centred, axis=-1, keepdims=True) + 1e-06)
+        unit_norm = centred * inv_std
+        normed = (unit_norm * gain + norm_bias).astype(jnp.bfloat16)
+        hidden = (
+            jnp.dot(normed, in_weight_ref[...], preferred_element_type=jnp.float32) + in_bias_ref[...]
+        )
+        act_full, gelu_slope = gelu_parts(hidden)
+        activation = act_full.astype(jnp.bfloat16)
+        branch = (
+            jnp.dot(activation, out_weight_ref[...], preferred_element_type=jnp.float32) + out_bias
+        )
+        centre = image_ref[span].astype(jnp.float32).reshape(pixels, channels)
+        output_ref[span] = (
+            (centre + layer_scale * branch).astype(jnp.bfloat16).reshape(CHUNK, n_cols, channels)
+        )
+        cot_full = cot_ref[span].astype(jnp.float32).reshape(pixels, channels)
+        scaled = (cot_full * layer_scale).astype(jnp.bfloat16)
+        d_act = jnp.dot(scaled, out_weight_t_ref[...], preferred_element_type=jnp.float32)
+        d_hidden_full = d_act * gelu_slope
+        d_hidden = d_hidden_full.astype(jnp.bfloat16)
+        d_normed = jnp.dot(d_hidden, in_weight_t_ref[...], preferred_element_type=jnp.float32)
+        d_unit = d_normed * gain
+        d_conv = (
+            d_unit
+            - jnp.mean(d_unit, axis=-1, keepdims=True)
+            - unit_norm * jnp.mean(d_unit * unit_norm, axis=-1, keepdims=True)
+        ) * inv_std
+        d_conv_3 = d_conv.reshape(CHUNK, n_cols, channels)
+        d_main_ref[span] = d_conv_3[:, :, 0:128]
+        d_rest_ref[span] = jnp.concatenate(
+            [d_conv_3[:, 0:96, 128:192], d_conv_3[:, 96:192, 128:192]], axis=2
+        )
+        d_conv_ref[span] = d_conv_3.astype(jnp.bfloat16)
+        contract = (((0,), (0,)), ((), ()))
+        g_in_ref[...] += lax.dot_general(
+            normed, d_hidden, contract, preferred_element_type=jnp.float32
+        )
+        g_out_ref[...] += lax.dot_general(
+            scaled, activation, contract, preferred_element_type=jnp.float32
+        )
+        bias_sum_ref[...] += fold(d_hidden_full)
+        sums_ref[0] += fold(d_conv)
+        sums_ref[1] += fold(d_normed * unit_norm)
+        sums_ref[2] += fold(d_normed)
+        sums_ref[3] += fold(cot_full)
+        sums_ref[4] += fold(cot_full * branch)
+        return carry
+
+    lax.fori_loop(0, n_rows // CHUNK, chunk, 0)
+    tap_sums(main_ref, rest_ref, d_main_ref, d_rest_ref, tap_ref)
+
+    s_ref[...] = jnp.zeros_like(s_ref)
+    taps = jnp.sum(tap_ref[...], axis=1)
+    s_ref[0:49, 0:128] = taps[:, 0:128]
+    s_ref[0:49, 128:192] = taps[:, 128:192] + taps[:, 192:256]
+    s_ref[49:54, 0:channels] = jnp.sum(sums_ref[...], axis=1)
+    s_ref[52:53, 0:channels] = s_ref[52:53, 0:channels] * rows_ref[4:5]
+    bias_sum = jnp.sum(bias_sum_ref[...], axis=0, keepdims=True)
+    for k in range(4):
+        s_ref[54 + k : 55 + k, 0:channels] = bias_sum[:, channels * k : channels * (k + 1)]
+    w_ref[:, 0:channels] = g_in_ref[...].T
+    w_ref[:, channels : 2 * channels] = g_out_ref[...].T
+
+
+VMEM_LIMIT = 64 * 1024 * 1024 - 65536
+
+
+def block(padded, image, cotangent, taps, rows, in_weight, in_bias, out_weight):
+    n_rows, n_cols, channels = image.shape
+    hidden_units = in_weight.shape[1]
+    vmem = pl.BlockSpec(memory_space=pltpu.VMEM)
+    f32 = jnp.float32
+    return pl.pallas_call(
+        block_kernel,
+        out_shape=(
+            jax.ShapeDtypeStruct(image.shape, jnp.bfloat16),
+            jax.ShapeDtypeStruct(image.shape, jnp.bfloat16),
+            jax.ShapeDtypeStruct((hidden_units, 2 * channels), f32),
+            jax.ShapeDtypeStruct((64, 256), f32),
+        ),
+        in_specs=[vmem] * 10,
+        out_specs=(vmem,) * 4,
+        scratch_shapes=[
+            pltpu.VMEM((n_rows + 6, 200, 128), f32),
+            pltpu.VMEM((n_rows + 6, 104, 128), f32),
+            pltpu.VMEM((n_rows, n_cols, channels), f32),
+            pltpu.VMEM((n_rows, n_cols, 128), f32),
+            pltpu.VMEM((n_rows, n_cols // 2, 128), f32),
+            pltpu.VMEM((5, 8, channels), f32),
+            pltpu.VMEM((49, 8, 256), f32),
+            pltpu.VMEM((8, hidden_units), f32),
+            pltpu.VMEM((channels, hidden_units), f32),
+            pltpu.VMEM((channels, hidden_units), f32),
+        ],
+        compiler_params=pltpu.CompilerParams(vmem_limit_bytes=VMEM_LIMIT),
+    )(
+        padded,
+        image,
+        cotangent,
+        taps,
+        rows,
+        in_weight,
+        in_weight.T,
+        in_bias[None],
+        out_weight,
+        out_weight.T,
+    )
+
+
+def transposed_kernel(padded_ref, cot_ref, taps_ref, out_ref, main_ref, rest_ref, conv_ref):
+    widen(padded_ref, main_ref, rest_ref)
+
+    convolve(main_ref, rest_ref, taps_ref, True, conv_ref)
+
+    def step(i, carry):
+        out_ref[i] = (cot_ref[i].astype(jnp.float32) + conv_ref[i]).astype(jnp.bfloat16)
+        return carry
+
+    lax.fori_loop(0, cot_ref.shape[0], step, 0)
+
+
+def transposed_conv(d_padded, cotangent, taps):
     n_rows, n_cols, channels = cotangent.shape
-    pixels = n_rows * n_cols
-    hidden_units = in_weight.shape[1]
-    conv_out = depthwise(padded, conv_kernel, n_rows, n_cols) + conv_bias
-    average = jnp.mean(conv_out, axis=-1, keepdims=True)
-    centred = conv_out - average
-    inv_std = lax.rsqrt(jnp.mean(centred * centred, axis=-1, keepdims=True) + 1e-06)
-    unit_norm = centred * inv_std
-    normed = (unit_norm * norm_gain + norm_bias).astype(jnp.bfloat16)
-    hidden = (
-        jnp.dot(normed.reshape(pixels, channels), in_weight, preferred_element_type=jnp.float32)
-        + in_bias
-    )
-    act_full, gelu_slope = gelu_parts(hidden)
-    activation = act_full.astype(jnp.bfloat16)
-    branch = jnp.dot(activation, out_weight, preferred_element_type=jnp.float32) + out_bias
-    centre = padded[3 : 3 + n_rows, 3 : 3 + n_cols].astype(jnp.float32).reshape(pixels, channels)
-    output = (centre + layer_scale * branch).astype(jnp.bfloat16).reshape(n_rows, n_cols, channels)
-    cot_full = cotangent.astype(jnp.float32).reshape(pixels, channels)
-    scaled = (cot_full * layer_scale).astype(jnp.bfloat16)
-    d_act = lax.dot_general(
-        scaled, out_weight, (((1,), (1,)), ((), ())), preferred_element_type=jnp.float32
-    )
-    d_hidden_full = d_act * gelu_slope
-    d_hidden = d_hidden_full.astype(jnp.bfloat16)
-    d_normed = lax.dot_general(
-        d_hidden, in_weight, (((1,), (1,)), ((), ())), preferred_element_type=jnp.float32
-    )
-    d_normed = d_normed.reshape(n_rows, n_cols, channels)
-    d_unit = d_normed * norm_gain
-    d_conv = (
-        d_unit
-        - jnp.mean(d_unit, axis=-1, keepdims=True)
-        - unit_norm * jnp.mean(d_unit * unit_norm, axis=-1, keepdims=True)
-    ) * inv_std
-    shape_c = (n_rows, n_cols, channels)
-    shape_h = (n_rows, n_cols, hidden_units)
-    return (
-        output,
-        d_conv,
-        unit_norm,
-        normed,
-        activation.reshape(shape_h),
-        scaled.reshape(shape_c),
-        d_hidden.reshape(shape_h),
-        d_hidden_full.reshape(shape_h),
-        d_normed,
-        branch.reshape(shape_c),
-        cot_full.reshape(shape_c),
-    )
-
-
-def partials(results, padded, offset, n_rows, n_cols, layer_scale):
-    (
-        output,
-        d_conv,
-        unit_norm,
-        normed,
-        activation,
-        scaled,
-        d_hidden,
-        d_hidden_full,
-        d_normed,
-        branch,
-        cot_full,
-    ) = results
-
-    def interior(array):
-        return array.reshape(n_rows * n_cols, array.shape[2])
-
-    tap_sums = []
-    for row_tap in range(7):
-        for col_tap in range(7):
-            shifted = padded[
-                offset + row_tap : offset + row_tap + n_rows,
-                offset + col_tap : offset + col_tap + n_cols,
-            ].astype(jnp.float32)
-            tap_sums.append(jnp.sum(shifted * d_conv, axis=(0, 1)))
-    g_kernel = jnp.stack(tap_sums).reshape(7, 7, d_conv.shape[2])
-    g_conv_bias = jnp.sum(d_conv, axis=(0, 1))
-    g_gain = jnp.sum(interior(d_normed) * interior(unit_norm), axis=0)
-    g_norm_bias = jnp.sum(interior(d_normed), axis=0)
-    g_in_weight = lax.dot_general(
-        interior(normed),
-        interior(d_hidden),
-        (((0,), (0,)), ((), ())),
-        preferred_element_type=jnp.float32,
-    )
-    g_in_bias = jnp.sum(interior(d_hidden_full), axis=0)
-    g_out_weight = lax.dot_general(
-        interior(activation),
-        interior(scaled),
-        (((0,), (0,)), ((), ())),
-        preferred_element_type=jnp.float32,
-    )
-    g_out_bias = jnp.sum(interior(cot_full), axis=0) * layer_scale
-    g_scale = jnp.sum(interior(cot_full) * interior(branch), axis=0)
-    return (
-        g_kernel,
-        g_conv_bias,
-        g_gain,
-        g_norm_bias,
-        g_in_weight,
-        g_in_bias,
-        g_out_weight,
-        g_out_bias,
-        g_scale,
-    )
+    vmem = pl.BlockSpec(memory_space=pltpu.VMEM)
+    return pl.pallas_call(
+        transposed_kernel,
+        out_shape=jax.ShapeDtypeStruct(cotangent.shape, jnp.bfloat16),
+        in_specs=[vmem] * 3,
+        out_specs=vmem,
+        scratch_shapes=[
+            pltpu.VMEM((n_rows + 6, 200, 128), jnp.float32),
+            pltpu.VMEM((n_rows + 6, 104, 128), jnp.float32),
+            pltpu.VMEM((n_rows, n_cols, channels), jnp.float32),
+        ],
+        compiler_params=pltpu.CompilerParams(vmem_limit_bytes=VMEM_LIMIT),
+    )(d_padded, cotangent, taps)
 
 
 MESH = pl.DeviceIdType.MESH
@@ -467,53 +573,18 @@
     cotangent,
 ):
     n_rows, n_cols, channels = image.shape
-    padded = padded_2(image, (("rows", 0), ("cols", 1)), 3)
-    results = layer_pass(
-        padded,
-        cotangent,
-        conv_kernel,
-        conv_bias,
-        norm_gain,
-        norm_bias,
-        in_weight,
-        in_bias,
-        out_weight,
-        out_bias,
-        layer_scale,
+    hidden_units = in_weight.shape[1]
+    factor = 1.0 / math.sqrt(n_rows * lax.axis_size("rows") * n_cols * lax.axis_size("cols"))
+    sides = (("rows", 0), ("cols", 1))
+    taps = conv_kernel.reshape(49, channels)
+    taps = jnp.concatenate([taps, taps[:, 128:]], axis=1)
+    rows = jnp.stack([conv_bias, norm_gain, norm_bias, out_bias, layer_scale])
+    rows = jnp.pad(rows, ((0, 3), (0, 0)))
+    padded = padded_2(image, sides, 3)
+    output, d_conv, w_sum, s_sum = block(
+        padded, image, cotangent, taps, rows, in_weight, in_bias, out_weight
     )
-    output = results[0]
-    d_padded = padded_2(results[1].astype(jnp.bfloat16), (("rows", 0), ("cols", 1)), 3)
-    grad_terms = partials(results, padded, 0, n_rows, n_cols, layer_scale)
-    grad_image = (
-        cotangent.astype(jnp.float32) + transposed(d_padded, conv_kernel, n_rows, n_cols)
-    ).astype(jnp.bfloat16)
-    (
-        g_kernel,
-        g_conv_bias,
-        g_gain,
-        g_norm_bias,
-        g_in_weight,
-        g_in_bias,
-        g_out_weight,
-        g_out_bias,
-        g_scale,
-    ) = grad_terms
-    factor = 1.0 / math.sqrt(n_rows * lax.axis_size("rows") * n_cols * lax.axis_size("cols"))
-    hidden_units = in_weight.shape[1]
-    w_sum = jnp.concatenate([g_in_weight.T, g_out_weight], axis=1)
-    s_sum = jnp.concatenate(
-        [
-            g_kernel.reshape(49, channels),
-            g_conv_bias[None],
-            g_gain[None],
-            g_norm_bias[None],
-            g_out_bias[None],
-            g_scale[None],
-            g_in_bias.reshape(4, channels),
-        ],
-        axis=0,
-    )
-    s_sum = jnp.pad(s_sum, ((0, 6), (0, 64)))
+    grad_image = transposed_conv(padded_2(d_conv, sides, 3), cotangent, taps)
     w_share, s_all = reduce_all(w_sum, s_sum, factor)
     s_all = s_all[:, :channels]
     bias_all = s_all[54:58].reshape(hidden_units)

time: 261 us -> 152 us (0.58)
  other arithmetic: 127 us -> 7.41 us
  Pallas kernels: 42 us -> 100 us
  matrix products: 29 us -> 0 us
  local copies, waits for them, and re-layouts: 34.6 us -> 12.8 us
  waiting for transfers between devices: 3.21 us -> 8.66 us
    reduce_sum x12 -> x0, other arithmetic: 81.3 us -> none  [the longest x8 42.4 us: partials(): tap_sums.append(jnp.sum(shifted * d_conv, axis=(0, 1)))]
    pallas_call x0 -> x2, Pallas kernels: none -> 55.4 us  [the longest x1 38.9 us: block(): pl.pallas_call(block_kernel, out_shape=(jax.ShapeDtypeStruct(image.shape,...]
    convert_element_type x2 -> x0, other arithmetic: 38.6 us -> none  [the longest x1 36.7 us: body(): grad_image = (cotangent.astype(jnp.float32) + transposed(d_padded, conv_k...]
    dot_general x6 -> x0, matrix products: 29 us -> none  [the longest x1 6.05 us: layer_pass(): lax.dot_general(scaled, out_weight, (((1,), (1,)), ((), ())), preferred_e...]
    reshape x5 -> x1, local copies, waits for them, and re-layouts: 11.6 us -> 0.83 us  [body(): taps = conv_kernel.reshape(49, channels)]
    concatenate x1 -> x0, local copies, waits for them, and re-layouts: 5.34 us -> none  [body(): jnp.concatenate([g_kernel.reshape(49, channels), g_conv_bias[None], g_gai...]
    slice x3 -> x1, local copies, waits for them, and re-layouts: 4.14 us -> 0.01 us  [body(): taps = jnp.concatenate([taps, taps[:, 128:]], axis=1)]
    concatenate x1 -> x2, other arithmetic: 2.63 us -> 6.71 us  [padded_2(): shard = jnp.concatenate([before, shard, after], axis=dim)]
  transfers between devices with their start and end apart: 8 -> 8, of which waited for: 1 -> 3; matrix products, arithmetic and copies ran while one was open for 21% -> 6% of each run, Pallas kernels for 16% -> 29%
where the time goes in v2:
time: 152 us
  Pallas kernels  100 us (66%)
  starting transfers between devices  21.9 us (14%)
  local copies, waits for them, and re-layouts  12.8 us (8%)
  waiting for transfers between devices  8.66 us (6%)
  other arithmetic  7.41 us (5%)
    pallas_call x1, Pallas kernels, reduce_all(): pl.pallas_call(functools.partial(reduce_kernel, factor), out_shape=(jax.S...  44.7 us
    pallas_call x1, Pallas kernels, block(): pl.pallas_call(block_kernel, out_shape=(jax.ShapeDtypeStruct(image.shape,...  38.9 us
    pallas_call x1, Pallas kernels, transposed_conv(): pl.pallas_call(transposed_kernel, out_shape=jax.ShapeDtypeStruct(cotangen...  16.5 us
    ppermute x4, starting transfers between devices, padded_2(): before = lax.ppermute(last, axis, up)  15.5 us
    concatenate x2, other arithmetic, padded_2(): shard = jnp.concatenate([before, shard, after], axis=dim)  6.71 us
    ppermute x4, starting transfers between devices, padded_2(): after = lax.ppermute(first, axis, down)  6.43 us
    ppermute x4, waiting for transfers between devices, padded_2(): after = lax.ppermute(first, axis, down)  5.14 us
    unnamed x28, local copies, waits for them, and re-layouts  4.97 us
  transfers between devices with their start and end apart: 8, of which 3 were waited for; matrix products, arithmetic and copies ran while one was open for 6% of the time, Pallas kernels for 29%

profile of v2, /device:TPU:1, one launch (start us, length us, event | category | flops | bytes accessed | tf_op | source)
XLA Modules:
  0.0 151.7 jit_solution(12107282769081264985)
XLA Ops:
  0.7 1.2 fusion.3
  1.9 4.0 %collective-permute-start = (bf16[3,192,192]{2,1,0:T(8,128)(2,1)S(1)}, bf16[3,192,192]{2,1,0:T(8,128)(2,1)S(1)}, u32[]{:S(2)}, u32[]{:S(2)}) collective-permute-start(bf16[3,192,192]{2,1,0:T(8,128)(2,1)S(1)} %get-tuple-element.30), channel_id=1, source_target_pairs={{0,8},{8,16},{16,24},{24,32},{32,40},{40,48},{48,56},{56,64},{64,7... | collective-permute-start | bytes 663560 | tf_op jit(solution)/shard_map/ppermute | solution.py:19
  5.8 1.3 collective-permute-start.1
  7.1 0.8 reshape.31
  8.0 3.5 %collective-permute-done = bf16[3,192,192]{2,1,0:T(8,128)(2,1)S(1)} collective-permute-done((bf16[3,192,192]{2,1,0:T(8,128)(2,1)S(1)}, bf16[3,192,192]{2,1,0:T(8,128)(2,1)S(1)}, u32[]{:S(2)}, u32[]{:S(2)}) %collective-permute-start) | collective-permute-done | bytes 221216 | tf_op jit(solution)/shard_map/ppermute | solution.py:19
  11.6 0.1 constant_dynamic-update-slice_fusion.1
  11.7 3.6 %collective-permute-done.1 = bf16[3,192,192]{2,1,0:T(8,128)(2,1)S(1)} collective-permute-done((bf16[3,192,192]{2,1,0:T(8,128)(2,1)S(1)}, bf16[3,192,192]{2,1,0:T(8,128)(2,1)S(1)}, u32[]{:S(2)}, u32[]{:S(2)}) %collective-permute-start.1) | collective-permute-done | bytes 221216 | tf_op jit(solution)/shard_map/ppermute | solution.py:20
  15.4 1.4 copy-done.1
  16.8 4.9 %collective-permute-start.2 = (bf16[22,3,192]{2,1,0:T(4,128)(2,1)S(1)}, bf16[22,3,192]{2,1,0:T(4,128)(2,1)S(1)}, u32[]{:S(2)}, u32[]{:S(2)}) collective-permute-start(bf16[22,3,192]{2,1,0:T(4,128)(2,1)S(1)} %get-tuple-element.25), channel_id=1, source_target_pairs={{0,1},{1,2},{2,3},{3,4},{4,5},{5,6},{6,7},{8,9},{9,10},{10,11},{11... | collective-permute-start | bytes 76040 | tf_op jit(solution)/shard_map/ppermute | solution.py:19
  21.7 1.9 %collective-permute-start.3 = (bf16[22,3,192]{2,1,0:T(4,128)(2,1)S(1)}, bf16[22,3,192]{2,1,0:T(4,128)(2,1)S(1)}, u32[]{:S(2)}, u32[]{:S(2)}) collective-permute-start(bf16[22,3,192]{2,1,0:T(4,128)(2,1)S(1)} %get-tuple-element.26), channel_id=1, source_target_pairs={{1,0},{2,1},{3,2},{4,3},{5,4},{6,5},{7,6},{9,8},{10,9},{11,10},{12... | collective-permute-start | bytes 76040 | tf_op jit(solution)/shard_map/ppermute | solution.py:20
  23.6 0.7 pad_maximum_fusion.2.taps_ref
  24.3 0.6 broadcast_in_dim.3.in_bias_ref
  24.9 0.9 copy.22
  25.8 0.9 copy.23.out_weight_ref
  26.8 0.6 pad.4.rows_ref
  27.4 4.4 %pad_maximum_fusion.padded_ref = bf16[22,198,192]{2,1,0:T(8,128)(2,1)} fusion(bf16[22,3,192]{2,1,0:T(4,128)(2,1)S(1)} %collective-permute-done.3, bf16[22,192,192]{2,1,0:T(8,128)(2,1)} %copy-done.1, bf16[22,3,192]{2,1,0:T(4,128)(2,1)S(1)} %collective-permute-done.2), kind=kLoop, calls=%fused_computation | loop fusion | flops 5018112 | bytes 3345408 | tf_op jit(solution)/shard_map/concatenate | solution.py:21
  31.8 38.9 %shard_map.194 = (bf16[16,192,192]{2,1,0:T(8,128)(2,1)}, bf16[16,192,192]{2,1,0:T(8,128)(2,1)}, f32[768,384]{1,0:T(8,128)}, f32[64,256]{1,0:T(8,128)}) custom-call(bf16[22,198,192]{2,1,0:T(8,128)(2,1)} %pad_maximum_fusion.padded_ref, bf16[16,192,192]{2,1,0:T(8,128)(2,1)} %image_ref.1, bf16[16,192,192]{2,1,0:T(8,128)(2,1)} %cot_ref.3, ...), custom_call_target="tpu_custom_call" | custom-call | tf_op jit(solution)/shard_map/pallas_call | solution.py:216
  70.7 1.1 fusion.2
  71.8 1.3 collective-permute-start.5
  73.1 4.0 %collective-permute-start.4 = (bf16[3,192,192]{2,1,0:T(8,128)(2,1)S(1)}, bf16[3,192,192]{2,1,0:T(8,128)(2,1)S(1)}, u32[]{:S(2)}, u32[]{:S(2)}) collective-permute-start(bf16[3,192,192]{2,1,0:T(8,128)(2,1)S(1)} %get-tuple-element.28), channel_id=1, source_target_pairs={{0,8},{8,16},{16,24},{24,32},{32,40},{40,48},{48,56},{56,64},{64,7... | collective-permute-start | bytes 663560 | tf_op jit(solution)/shard_map/ppermute | solution.py:19
  77.1 44.7 %shard_map.196 = (f32[24,384]{1,0:T(8,128)}, f32[64,256]{1,0:T(8,128)}) custom-call(f32[768,384]{1,0:T(8,128)} %get-tuple-element.19.w_ref, f32[64,256]{1,0:T(8,128)} %get-tuple-element.20.s_ref), custom_call_target="tpu_custom_call" | custom-call | tf_op jit(solution)/shard_map/pallas_call | solution.py:529
  121.8 1.5 fusion.5
  123.3 1.5 %constant_dynamic-update-slice_fusion.4 = bf16[22,192,192]{2,1,0:T(8,128)(2,1)S(1)} fusion(bf16[22,192,192]{2,1,0:T(8,128)(2,1)S(1)} %constant_dynamic-update-slice_fusion.5, bf16[16,192,192]{2,1,0:T(8,128)(2,1)} %get-tuple-element.18), kind=kLoop, calls=%fused_computation.8 | loop fusion | bytes 2752512
  124.9 2.6 %collective-permute-start.6 = (bf16[22,3,192]{2,1,0:T(4,128)(2,1)S(1)}, bf16[22,3,192]{2,1,0:T(4,128)(2,1)S(1)}, u32[]{:S(2)}, u32[]{:S(2)}) collective-permute-start(bf16[22,3,192]{2,1,0:T(4,128)(2,1)S(1)} %get-tuple-element.23), channel_id=1, source_target_pairs={{0,1},{1,2},{2,3},{3,4},{4,5},{5,6},{6,7},{8,9},{9,10},{10,11},{11... | collective-permute-start | bytes 76040 | tf_op jit(solution)/shard_map/ppermute | solution.py:19
  127.5 1.9 %collective-permute-start.7 = (bf16[22,3,192]{2,1,0:T(4,128)(2,1)S(1)}, bf16[22,3,192]{2,1,0:T(4,128)(2,1)S(1)}, u32[]{:S(2)}, u32[]{:S(2)}) collective-permute-start(bf16[22,3,192]{2,1,0:T(4,128)(2,1)S(1)} %get-tuple-element.24), channel_id=1, source_target_pairs={{1,0},{2,1},{3,2},{4,3},{5,4},{6,5},{7,6},{9,8},{10,9},{11,10},{12... | collective-permute-start | bytes 76040 | tf_op jit(solution)/shard_map/ppermute | solution.py:20
  129.5 0.6 fusion.4
  130.1 0.1 reshape.33
  130.1 0.6 reshape.32
  130.8 0.6 dynamic_slice.3
  131.3 1.5 %collective-permute-done.7 = bf16[22,3,192]{2,1,0:T(4,128)(2,1)S(1)} collective-permute-done((bf16[22,3,192]{2,1,0:T(4,128)(2,1)S(1)}, bf16[22,3,192]{2,1,0:T(4,128)(2,1)S(1)}, u32[]{:S(2)}, u32[]{:S(2)}) %collective-permute-start.7) | collective-permute-done | bytes 25376 | tf_op jit(solution)/shard_map/ppermute | solution.py:20
  132.9 2.4 %pad_maximum_fusion.1.padded_ref = bf16[22,198,192]{2,1,0:T(8,128)(2,1)} fusion(bf16[22,3,192]{2,1,0:T(4,128)(2,1)S(1)} %collective-permute-done.7, bf16[22,192,192]{2,1,0:T(8,128)(2,1)S(1)} %constant_dynamic-update-slice_fusion.3, bf16[22,3,192]{2,1,0:T(4,128)(2,1)S(1)} %collective-permute-done.6), kind=kLoop, calls=%fused_computation.1 | loop fusion | flops 5018112 | bytes 3345408 | tf_op jit(solution)/shard_map/concatenate | solution.py:21
  135.2 16.5 %shard_map.195 = bf16[16,192,192]{2,1,0:T(8,128)(2,1)} custom-call(bf16[22,198,192]{2,1,0:T(8,128)(2,1)} %pad_maximum_fusion.1.padded_ref, bf16[16,192,192]{2,1,0:T(8,128)(2,1)} %cot_ref.3, f32[49,256]{1,0:T(8,128)} %pad_maximum_fusion.2.taps_ref), custom_call_target="tpu_custom_call" | custom-call | tf_op jit(solution)/shard_map/pallas_call | solution.py:268
  (36 shorter events, 0.3 us)
Async XLA Ops:
  0.6 10.9 %copy-start = (bf16[16,192,192]{2,1,0:T(8,128)(2,1)S(1)}, bf16[16,192,192]{2,1,0:T(8,128)(2,1)}, u32[]{:S(2)}) copy-start(bf16[16,192,192]{2,1,0:T(8,128)(2,1)} %image_ref.1) | copy-start | bytes 3538948
  1.9 9.6 %collective-permute-start = (bf16[3,192,192]{2,1,0:T(8,128)(2,1)S(1)}, bf16[3,192,192]{2,1,0:T(8,128)(2,1)S(1)}, u32[]{:S(2)}, u32[]{:S(2)}) collective-permute-start(bf16[3,192,192]{2,1,0:T(8,128)(2,1)S(1)} %get-tuple-element.30), channel_id=1, source_target_pairs={{0,8},{8,16},{16,24},{24,32},{32,40},{40,48},{48,56},{56,64},{64,7... | collective-permute-start | bytes 663560 | tf_op jit(solution)/shard_map/ppermute | solution.py:19
  5.8 9.5 %collective-permute-start.1 = (bf16[3,192,192]{2,1,0:T(8,128)(2,1)S(1)}, bf16[3,192,192]{2,1,0:T(8,128)(2,1)S(1)}, u32[]{:S(2)}, u32[]{:S(2)}) collective-permute-start(bf16[3,192,192]{2,1,0:T(8,128)(2,1)S(1)} %get-tuple-element.29), channel_id=1, source_target_pairs={{8,0},{16,8},{24,16},{32,24},{40,32},{48,40},{56,48},{64,56},{72,6... | collective-permute-start | bytes 663560 | tf_op jit(solution)/shard_map/ppermute | solution.py:20
  11.5 12.8 %copy-start.5 = (f32[768]{0:T(1024)S(1)}, f32[768]{0:T(1024)}, u32[]{:S(2)}) copy-start(f32[768]{0:T(1024)} %param.17) | copy-start | bytes 9220
  11.5 13.4 %copy-start.2 = (bf16[192,768]{1,0:T(8,128)(2,1)S(1)}, bf16[192,768]{1,0:T(8,128)(2,1)}, u32[]{:S(2)}) copy-start(bf16[192,768]{1,0:T(8,128)(2,1)} %in_weight_ref.1) | copy-start | bytes 884740
  11.5 14.3 %copy-start.3 = (bf16[768,192]{0,1:T(8,128)(2,1)S(1)}, bf16[768,192]{0,1:T(8,128)(2,1)}, u32[]{:S(2)}) copy-start(bf16[768,192]{0,1:T(8,128)(2,1)} %param.18) | copy-start | bytes 884740
  11.6 15.2 %copy-start.6 = (f32[192]{0:T(256)S(1)}, f32[192]{0:T(256)}, u32[]{:S(2)}) copy-start(f32[192]{0:T(256)} %param.13) | copy-start | bytes 2308
  11.6 15.2 %copy-start.7 = (f32[192]{0:T(256)S(1)}, f32[192]{0:T(256)}, u32[]{:S(2)}) copy-start(f32[192]{0:T(256)} %param.14) | copy-start | bytes 2308
  11.6 15.2 %copy-start.8 = (f32[192]{0:T(256)S(1)}, f32[192]{0:T(256)}, u32[]{:S(2)}) copy-start(f32[192]{0:T(256)} %param.15) | copy-start | bytes 2308
  11.6 15.2 %copy-start.9 = (f32[192]{0:T(256)S(1)}, f32[192]{0:T(256)}, u32[]{:S(2)}) copy-start(f32[192]{0:T(256)} %param.19) | copy-start | bytes 2308
  11.6 15.2 %copy-start.10 = (f32[192]{0:T(256)S(1)}, f32[192]{0:T(256)}, u32[]{:S(2)}) copy-start(f32[192]{0:T(256)} %param.20) | copy-start | bytes 2308
  15.4 1.4 copy-start.1
  16.8 10.7 %collective-permute-start.2 = (bf16[22,3,192]{2,1,0:T(4,128)(2,1)S(1)}, bf16[22,3,192]{2,1,0:T(4,128)(2,1)S(1)}, u32[]{:S(2)}, u32[]{:S(2)}) collective-permute-start(bf16[22,3,192]{2,1,0:T(4,128)(2,1)S(1)} %get-tuple-element.25), channel_id=1, source_target_pairs={{0,1},{1,2},{2,3},{3,4},{4,5},{5,6},{6,7},{8,9},{9,10},{10,11},{11... | collective-permute-start | bytes 76040 | tf_op jit(solution)/shard_map/ppermute | solution.py:19
  21.7 5.8 %collective-permute-start.3 = (bf16[22,3,192]{2,1,0:T(4,128)(2,1)S(1)}, bf16[22,3,192]{2,1,0:T(4,128)(2,1)S(1)}, u32[]{:S(2)}, u32[]{:S(2)}) collective-permute-start(bf16[22,3,192]{2,1,0:T(4,128)(2,1)S(1)} %get-tuple-element.26), channel_id=1, source_target_pairs={{1,0},{2,1},{3,2},{4,3},{5,4},{6,5},{7,6},{9,8},{10,9},{11,10},{12... | collective-permute-start | bytes 76040 | tf_op jit(solution)/shard_map/ppermute | solution.py:20
  71.8 53.1 %collective-permute-start.5 = (bf16[3,192,192]{2,1,0:T(8,128)(2,1)S(1)}, bf16[3,192,192]{2,1,0:T(8,128)(2,1)S(1)}, u32[]{:S(2)}, u32[]{:S(2)}) collective-permute-start(bf16[3,192,192]{2,1,0:T(8,128)(2,1)S(1)} %get-tuple-element.27), channel_id=1, source_target_pairs={{8,0},{16,8},{24,16},{32,24},{40,32},{48,40},{56,48},{64,56},{72,6... | collective-permute-start | bytes 663560 | tf_op jit(solution)/shard_map/ppermute | solution.py:20
  73.1 50.2 %collective-permute-start.4 = (bf16[3,192,192]{2,1,0:T(8,128)(2,1)S(1)}, bf16[3,192,192]{2,1,0:T(8,128)(2,1)S(1)}, u32[]{:S(2)}, u32[]{:S(2)}) collective-permute-start(bf16[3,192,192]{2,1,0:T(8,128)(2,1)S(1)} %get-tuple-element.28), channel_id=1, source_target_pairs={{0,8},{8,16},{16,24},{24,32},{32,40},{40,48},{48,56},{56,64},{64,7... | collective-permute-start | bytes 663560 | tf_op jit(solution)/shard_map/ppermute | solution.py:19
  123.3 6.2 %copy-start.4 = (f32[64,256]{1,0:T(8,128)S(1)}, f32[64,256]{1,0:T(8,128)}, u32[]{:S(2)}) copy-start(f32[64,256]{1,0:T(8,128)} %get-tuple-element.21) | copy-start | bytes 196612
  124.9 6.4 %collective-permute-start.6 = (bf16[22,3,192]{2,1,0:T(4,128)(2,1)S(1)}, bf16[22,3,192]{2,1,0:T(4,128)(2,1)S(1)}, u32[]{:S(2)}, u32[]{:S(2)}) collective-permute-start(bf16[22,3,192]{2,1,0:T(4,128)(2,1)S(1)} %get-tuple-element.23), channel_id=1, source_target_pairs={{0,1},{1,2},{2,3},{3,4},{4,5},{5,6},{6,7},{8,9},{9,10},{10,11},{11... | collective-permute-start | bytes 76040 | tf_op jit(solution)/shard_map/ppermute | solution.py:19
  127.5 5.4 %collective-permute-start.7 = (bf16[22,3,192]{2,1,0:T(4,128)(2,1)S(1)}, bf16[22,3,192]{2,1,0:T(4,128)(2,1)S(1)}, u32[]{:S(2)}, u32[]{:S(2)}) collective-permute-start(bf16[22,3,192]{2,1,0:T(4,128)(2,1)S(1)} %get-tuple-element.24), channel_id=1, source_target_pairs={{1,0},{2,1},{3,2},{4,3},{5,4},{6,5},{7,6},{9,8},{10,9},{11,10},{12... | collective-permute-start | bytes 76040 | tf_op jit(solution)/shard_map/ppermute | solution.py:20

commit v3 on v0

v3 whole, which is shorter than its diff:
```python
import functools
import math

import jax
import jax.numpy as jnp
from jax import lax
from jax.experimental import pallas as pl
from jax.experimental.pallas import tpu as pltpu
from jax.sharding import PartitionSpec as P


def gelu_parts(hidden):
    normal_cdf = 0.5 * (1.0 + jax.scipy.special.erf(hidden * 0.7071067811865476))
    normal_pdf = jnp.exp(-0.5 * hidden * hidden) * 0.3989422804014327
    return (hidden * normal_cdf, normal_cdf + hidden * normal_pdf)


MESH = pl.DeviceIdType.MESH
SHARE = 24
CHUNK = 2
VMEM_LIMIT = 64 * 1024 * 1024 - 65536
SIDES = ((-1, 0), (1, 0), (0, -1), (0, 1), (-1, -1), (-1, 1), (1, -1), (1, 1))


def remote(source, target, send, recv, place):
    return pltpu.make_async_remote_copy(
        source, target, send, recv, device_id=place, device_id_type=MESH
    )


def halo_parts(block_ref, halo, k):
    top, bottom, left, right = halo
    d_row, d_col = SIDES[k]
    first, last = pl.ds(0, 16), pl.ds(176, 16)
    if d_col == 0:
        rows = pl.ds(0, 3) if d_row < 0 else pl.ds(13, 3)
        return block_ref.at[rows], bottom if d_row < 0 else top
    cols, side = (first, right) if d_col < 0 else (last, left)
    if d_row == 0:
        return block_ref.at[:, cols], side.at[pl.ds(3, 16)]
    if d_row < 0:
        return block_ref.at[pl.ds(0, 3), cols], side.at[pl.ds(19, 3)]
    return block_ref.at[pl.ds(13, 3), cols], side.at[pl.ds(0, 3)]


def inside(row, col):
    return (row >= 0) & (row < 32) & (col >= 0) & (col < 8)


def halo_send(block_ref, halo, sems, row, col, act):
    for k, (d_row, d_col) in enumerate(SIDES):
        source, target = halo_parts(block_ref, halo, k)

        @pl.when(inside(row + d_row, col + d_col))
        def _(k=k, d_row=d_row, d_col=d_col, source=source, target=target):
            act(remote(source, target, sems.at[0, k], sems.at[1, k], (row + d_row, col + d_col)))


def halo_clear(block_ref, halo, row, col):
    for k, (d_row, d_col) in enumerate(SIDES):
        _, target = halo_parts(block_ref, halo, k)

        @pl.when(jnp.logical_not(inside(row - d_row, col - d_col)))
        def _(target=target):
            target[...] = jnp.zeros(target.shape, jnp.bfloat16)


def halo_wait(block_ref, halo, sems, row, col):
    for k, (d_row, d_col) in enumerate(SIDES):
        source, target = halo_parts(block_ref, halo, k)

        @pl.when(inside(row - d_row, col - d_col))
        def _(k=k, source=source, target=target):
            pltpu.make_async_copy(source, target, sems.at[1, k]).wait()


def widen(source_ref, main_ref, rest_ref, base):
    def step(i, carry):
        row = source_ref[i].astype(jnp.float32)
        row = jnp.concatenate(
            [jnp.zeros((3, 192), jnp.float32), row, jnp.zeros((5, 192), jnp.float32)], axis=0
        )
        main_ref[base + i] = row[:, 0:128]
        rest_ref[base + i] = jnp.concatenate([row[0:104, 128:192], row[96:200, 128:192]], axis=1)
        return carry

    lax.fori_loop(0, source_ref.shape[0], step, 0)


def join(source_ref, left_ref, right_ref, main_ref, rest_ref, base):
    def step(i, carry):
        first = jnp.concatenate(
            [
                left_ref[base + i].astype(jnp.float32)[13:16],
                source_ref[i, 0:16].astype(jnp.float32)[0:5],
            ],
            axis=0,
        )
        last = jnp.concatenate(
            [
                source_ref[i, 176:192].astype(jnp.float32)[13:16],
                right_ref[base + i].astype(jnp.float32)[0:3],
                jnp.zeros((2, 192), jnp.float32),
            ],
            axis=0,
        )
        main_ref[base + i, 0:8] = first[:, 0:128]
        main_ref[base + i, 192:200] = last[:, 0:128]
        rest_ref[base + i, 0:8, 0:64] = first[:, 128:192]
        rest_ref[base + i, 96:104, 64:128] = last[:, 128:192]
        return carry

    lax.fori_loop(0, source_ref.shape[0], step, 0)


def gather_rows(wide_ref, taps_ref, first, start, flip, accum, rows, outs):
    lo, hi = rows
    for b in range(7):
        shifted = wide_ref[lo:hi, pl.ds(start + b, 8), :]
        for a in range(7):
            tap = 48 - (7 * a + b) if flip else 7 * a + b
            begin, end = max(outs[0], lo - a), min(outs[1], hi - a)
            if begin >= end:
                continue
            part = shifted[begin + a - lo : end + a - lo] * taps_ref[tap, first : first + 128]
            part = accum[begin - outs[0] : end - outs[0]] + part
            pieces = [accum[: begin - outs[0]], part, accum[end - outs[0] :]]
            pieces = [piece for piece in pieces if piece.shape[0]]
            accum = jnp.concatenate(pieces, axis=0) if len(pieces) > 1 else pieces[0]
    return accum


def put_main(out_ref, start, rows, tile):
    out_ref[rows, pl.ds(start, 8), 0:128] = tile


def put_rest(out_ref, start, rows, tile):
    out_ref[rows, pl.ds(start, 8), 128:192] = tile[:, :, 0:64]
    out_ref[rows, pl.ds(start + 96, 8), 128:192] = tile[:, :, 64:128]


def take_main(out_ref, start, rows):
    return out_ref[rows, pl.ds(start, 8), 0:128]


def take_rest(out_ref, start, rows):
    return jnp.concatenate(
        [
            out_ref[rows, pl.ds(start, 8), 128:192],
            out_ref[rows, pl.ds(start + 96, 8), 128:192],
        ],
        axis=2,
    )


def tiles(wide_ref, taps_ref, first, flip, out_ref, put, rows, span, stride=1):
    def step(i, carry):
        start = pl.multiple_of(8 * stride * i, 8)
        accum = jnp.zeros((16, 8, 128), jnp.float32)
        accum = gather_rows(wide_ref, taps_ref, first, start, flip, accum, rows, (0, 16))
        put(out_ref, start, slice(0, 16), accum)
        return carry

    lax.fori_loop(span[0], span[1], step, 0)


def edge_rows(wide_ref, taps_ref, first, out_ref, take, put, span):
    def step(i, carry):
        start = pl.multiple_of(8 * i, 8)
        for rows, outs in (((0, 3), (0, 3)), ((19, 22), (13, 16))):
            where = slice(*outs)
            accum = take(out_ref, start, where)
            accum = gather_rows(wide_ref, taps_ref, first, start, False, accum, rows, outs)
            put(out_ref, start, where, accum)
        return carry

    lax.fori_loop(span[0], span[1], step, 0)


def tap_sums(wide_ref, d_ref, first, sums_ref, steps):
    n_rows = d_ref.shape[0]

    def step(i, carry):
        start = pl.multiple_of(8 * i, 8)
        d_tile = d_ref[:, pl.ds(start, 8), :]
        for b in range(7):
            shifted = wide_ref[:, pl.ds(start + b, 8), :]
            for a in range(7):
                tap = 7 * a + b
                sums_ref[tap, :, first : first + 128] += jnp.sum(
                    shifted[a : a + n_rows] * d_tile, axis=0
                )
        return carry

    lax.fori_loop(0, steps, step, 0)


def fold(values):
    return jnp.sum(values.reshape(values.shape[0] // 8, 8, values.shape[1]), axis=0)


def fused_kernel(
    factor,
    image_ref,
    cot_ref,
    kernel_ref,
    rows_ref,
    in_weight_ref,
    out_weight_ref,
    output_ref,
    grad_image_ref,
    g_kernel_ref,
    g_rows_ref,
    g_in_out_ref,
    g_bias_out_ref,
    g_out_out_ref,
    taps_ref,
    in_t_ref,
    out_t_ref,
    main_ref,
    rest_ref,
    conv_ref,
    d_main_ref,
    d_rest_ref,
    d_block_ref,
    top_ref,
    bottom_ref,
    left_ref,
    right_ref,
    d_top_ref,
    d_bottom_ref,
    d_left_ref,
    d_right_ref,
    sums_ref,
    tap_ref,
    bias_sum_ref,
    g_in_ref,
    g_out_ref,
    w_ref,
    s_ref,
    core_tx,
    core_rx,
    score_rx,
    row_tx,
    srow_tx,
    row_rx,
    srow_rx,
    col_rx,
    scol_rx,
    gat_tx,
    gat_rx,
    halo_sems,
    d_halo_sems,
    core_send,
    core_recv,
    row_send,
    row_recv,
    col_send,
    col_recv,
    gat_send,
    gat_recv,
):
    n_rows, n_cols, channels = image_ref.shape
    pixels = CHUNK * n_cols
    f32, bf16 = jnp.float32, jnp.bfloat16
    row = lax.axis_index("rows")
    col = lax.axis_index("cols")
    core = lax.rem(col, 2)
    pair = col - core
    other = pair + 1 - core
    half = row // 16
    place = lax.rem(row, 16)
    owner = half == core
    halo = (top_ref, bottom_ref, left_ref, right_ref)
    d_halo = (d_top_ref, d_bottom_ref, d_left_ref, d_right_ref)

    barrier = pltpu.get_barrier_semaphore()

    def greet_row(step, carry):
        peer = lax.rem(row + step, 32)
        pl.semaphore_signal(barrier, inc=1, device_id=(peer, col), device_id_type=MESH)
        return carry

    def greet_col(step, carry):
        peer = lax.rem(col + step, 8)
        pl.semaphore_signal(barrier, inc=1, device_id=(row, peer), device_id_type=MESH)
        return carry

    lax.fori_loop(1, 32, greet_row, 0)
    lax.fori_loop(1, 8, greet_col, 0)
    for d_row, d_col in SIDES[4:]:
        corner = (lax.rem(row + d_row + 32, 32), lax.rem(col + d_col + 8, 8))
        pl.semaphore_signal(barrier, inc=1, device_id=corner, device_id_type=MESH)

    halo_clear(image_ref, halo, row, col)
    halo_clear(d_block_ref, d_halo, row, col)
    for a in range(7):
        taps_ref[7 * a : 7 * a + 7, 0:192] = kernel_ref[a]
        taps_ref[7 * a : 7 * a + 7, 192:256] = kernel_ref[a][:, 128:192]
    widen(image_ref, main_ref, rest_ref, 3)
    own = (3, 19)
    tiles(rest_ref, taps_ref, 128, False, conv_ref, put_rest, own, (1, 11))
    pl.semaphore_wait(barrier, 42)
    halo_send(image_ref, halo, halo_sems, row, col, lambda copy: copy.start())
    tiles(main_ref, taps_ref, 0, False, conv_ref, put_main, own, (1, 23))
    in_t_ref[...] = in_weight_ref[...].astype(f32).T.astype(bf16)
    out_t_ref[...] = out_weight_ref[...].astype(f32).T.astype(bf16)
    sums_ref[...] = jnp.zeros_like(sums_ref)
    tap_ref[...] = jnp.zeros_like(tap_ref)
    bias_sum_ref[...] = jnp.zeros_like(bias_sum_ref)
    g_in_ref[...] = jnp.zeros_like(g_in_ref)
    g_out_ref[...] = jnp.zeros_like(g_out_ref)
    s_ref[...] = jnp.zeros_like(s_ref)
    halo_wait(image_ref, halo, halo_sems, row, col)

    def widen_all(block_ref, pieces, center):
        above, below, left, right = pieces
        for source, base in ((above, 0), (below, 19)) + (((block_ref, 3),) if center else ()):
            widen(source, main_ref, rest_ref, base)
        for source, base in ((above, 0), (block_ref, 3), (below, 19)):
            join(source, left, right, main_ref, rest_ref, base)

    widen_all(image_ref, halo, False)
    whole = (0, 22)
    edge_rows(main_ref, taps_ref, 0, conv_ref, take_main, put_main, (1, 23))
    edge_rows(rest_ref, taps_ref, 128, conv_ref, take_rest, put_rest, (1, 11))
    tiles(main_ref, taps_ref, 0, False, conv_ref, put_main, whole, (0, 2), 23)
    tiles(rest_ref, taps_ref, 128, False, conv_ref, put_rest, whole, (0, 2), 11)

    def chunk(i, carry):
        span = pl.ds(CHUNK * i, CHUNK)
        conv_bias, gain, norm_bias, out_bias, layer_scale = (
            rows_ref[k : k + 1, 0:channels] for k in range(5)
        )
        conv_out = conv_ref[span].reshape(pixels, channels) + conv_bias
        centred = conv_out - jnp.mean(conv_out, axis=-1, keepdims=True)
        inv_std = lax.rsqrt(jnp.mean(centred * centred, axis=-1, keepdims=True) + 1e-06)
        unit_norm = centred * inv_std
        normed = (unit_norm * gain + norm_bias).astype(bf16)
        hidden = jnp.dot(normed, in_weight_ref[...], preferred_element_type=f32) + rows_ref[5:6]
        act_full, gelu_slope = gelu_parts(hidden)
        activation = act_full.astype(bf16)
        branch = jnp.dot(activation, out_weight_ref[...], preferred_element_type=f32) + out_bias
        centre = image_ref[span].astype(f32).reshape(pixels, channels)
        output_ref[span] = (
            (centre + layer_scale * branch).astype(bf16).reshape(CHUNK, n_cols, channels)
        )
        cot_full = cot_ref[span].astype(f32).reshape(pixels, channels)
        scaled = (cot_full * layer_scale).astype(bf16)
        d_act = jnp.dot(scaled, out_t_ref[...], preferred_element_type=f32)
        d_hidden_full = d_act * gelu_slope
        d_hidden = d_hidden_full.astype(bf16)
        d_normed = jnp.dot(d_hidden, in_t_ref[...], preferred_element_type=f32)
        d_unit = d_normed * gain
        d_conv = (
            d_unit
            - jnp.mean(d_unit, axis=-1, keepdims=True)
            - unit_norm * jnp.mean(d_unit * unit_norm, axis=-1, keepdims=True)
        ) * inv_std
        d_conv_3 = d_conv.reshape(CHUNK, n_cols, channels)
        d_main_ref[span] = d_conv_3[:, :, 0:128]
        d_rest_ref[span] = jnp.concatenate(
            [d_conv_3[:, 0:96, 128:192], d_conv_3[:, 96:192, 128:192]], axis=2
        )
        d_block_ref[span] = d_conv_3.astype(bf16)
        contract = (((0,), (0,)), ((), ()))
        g_in_ref[...] += lax.dot_general(normed, d_hidden, contract, preferred_element_type=f32)
        g_out_ref[...] += lax.dot_general(scaled, activation, contract, preferred_element_type=f32)
        bias_sum_ref[...] += fold(d_hidden_full)
        sums_ref[0] += fold(d_conv)
        sums_ref[1] += fold(d_normed * unit_norm)
        sums_ref[2] += fold(d_normed)
        sums_ref[3] += fold(cot_full)
        sums_ref[4] += fold(cot_full * branch)
        return carry

    lax.fori_loop(0, n_rows // CHUNK, chunk, 0)
    halo_send(d_block_ref, d_halo, d_halo_sems, row, col, lambda copy: copy.start())

    w_ref[:, 0:channels] = g_in_ref[...].T
    w_ref[:, channels : 2 * channels] = g_out_ref[...].T

    def share_of(index):
        rows = w_ref[pl.ds(pl.multiple_of(index * SHARE, 8), SHARE), :]
        return jnp.concatenate([rows[:, 0:128], rows[:, 128:256], rows[:, 256:384]], axis=0)

    def pack_core(j, carry):
        core_tx[j] = share_of(16 * (1 - core) + j).astype(bf16)
        return carry

    lax.fori_loop(0, 16, pack_core, 0)
    to_core = remote(core_tx, core_rx, core_send.at[0], core_recv.at[0], (row, other))
    to_core_s = remote(s_ref, score_rx, core_send.at[1], core_recv.at[1], (row, other))
    to_core.start()

    tap_sums(rest_ref, d_rest_ref, 128, tap_ref, 12)
    to_core.wait()

    def row_copy(j):
        return remote(
            row_tx.at[j],
            row_rx.at[row],
            row_send.at[0, j],
            row_recv.at[0, row],
            (16 * core + j, col),
        )

    def s_row_copy(j):
        return remote(
            srow_tx.at[j],
            srow_rx.at[row],
            row_send.at[1, j],
            row_recv.at[1, row],
            (16 * core + j, col),
        )

    def col_copy(step):
        return remote(
            col_rx.at[col // 2],
            col_rx.at[col // 2],
            col_send.at[0, step],
            col_recv.at[0, col // 2],
            (row, lax.rem(col + step, 8)),
        )

    def s_col_copy(step):
        return remote(
            scol_rx.at[col // 2],
            scol_rx.at[col // 2],
            col_send.at[1, step],
            col_recv.at[1, col // 2],
            (row, lax.rem(col + step, 8)),
        )

    def gather_copy(step):
        peer = 16 * half + lax.rem(place + step, 16)
        return remote(
            gat_tx, gat_rx.at[place], gat_send.at[step], gat_recv.at[place], (peer, col)
        )

    def over_rows(act):
        def step(k, carry):
            j = lax.rem(place + k, 16)

            @pl.when(16 * core + j != row)
            def _():
                act(j)

            return carry

        lax.fori_loop(0, 16, step, 0)

    def over(first, last, act):
        def step(k, carry):
            act(k)
            return carry

        lax.fori_loop(first, last, step, 0)

    def pack_row(j, carry):
        row_tx[j] = (share_of(16 * core + j) + core_rx[j].astype(f32)).astype(bf16)
        return carry

    lax.fori_loop(0, 16, pack_row, 0)
    over_rows(lambda j: row_copy(j).start())

    tap_sums(main_ref, d_main_ref, 0, tap_ref, 24)
    taps = jnp.sum(tap_ref[...], axis=1)
    s_ref[0:49, 0:128] = taps[:, 0:128]
    s_ref[0:49, 128:192] = taps[:, 128:192] + taps[:, 192:256]
    s_ref[49:54, 0:channels] = jnp.sum(sums_ref[...], axis=1)
    s_ref[52:53, 0:channels] = s_ref[52:53, 0:channels] * rows_ref[4:5, 0:channels]
    bias_sum = jnp.sum(bias_sum_ref[...], axis=0, keepdims=True)
    for k in range(4):
        s_ref[54 + k : 55 + k, 0:channels] = bias_sum[:, channels * k : channels * (k + 1)]
    to_core_s.start()

    halo_wait(d_block_ref, d_halo, d_halo_sems, row, col)
    widen_all(d_block_ref, d_halo, True)
    tiles(rest_ref, taps_ref, 128, True, conv_ref, put_rest, whole, (0, 6))

    to_core_s.wait()
    for j in range(16):
        up, across = 8 * (j // 2), 128 * (j % 2)
        srow_tx[j] = (
            s_ref[up : up + 8, across : across + 128]
            + score_rx[up : up + 8, across : across + 128]
        )
    over_rows(lambda j: s_row_copy(j).start())

    @pl.when(owner)
    def _():
        row_rx[row] = row_tx[place]

        def wait_row(step):
            peer = lax.rem(row + step, 32)
            pltpu.make_async_copy(row_tx.at[0], row_rx.at[peer], row_recv.at[0, peer]).wait()

        over(1, 32, wait_row)

        def add_row(i, carry):
            return carry + row_rx[i].astype(f32)

        total = lax.fori_loop(0, 32, add_row, jnp.zeros((72, 128), f32))
        col_rx[col // 2] = total.astype(bf16)
        over(1, 8, lambda step: col_copy(step).start())

    tiles(main_ref, taps_ref, 0, True, conv_ref, put_main, whole, (0, 12))

    @pl.when(owner)
    def _():
        srow_rx[row] = srow_tx[place]

        def wait_row(step):
            peer = lax.rem(row + step, 32)
            pltpu.make_async_copy(srow_tx.at[0], srow_rx.at[peer], row_recv.at[1, peer]).wait()

        over(1, 32, wait_row)

        def add_row(i, carry):
            return carry + srow_rx[i]

        scol_rx[col // 2] = lax.fori_loop(0, 32, add_row, jnp.zeros((8, 128), f32))
        over(1, 8, lambda step: s_col_copy(step).start())

    tiles(main_ref, taps_ref, 0, True, conv_ref, put_main, whole, (12, 18))

    def wait_col(y):
        @pl.when(2 * y + half != col)
        def _():
            pltpu.make_async_copy(scol_rx.at[y], scol_rx.at[y], col_recv.at[1, y]).wait()

    over(0, 4, wait_col)
    gat_tx[...] = ((scol_rx[0] + scol_rx[1]) + (scol_rx[2] + scol_rx[3])) * factor
    over(1, 16, lambda step: gather_copy(step).start())

    tiles(main_ref, taps_ref, 0, True, conv_ref, put_main, whole, (18, 24))
    tiles(rest_ref, taps_ref, 128, True, conv_ref, put_rest, whole, (6, 12))

    def finish(i, carry):
        grad_image_ref[i] = (cot_ref[i].astype(f32) + conv_ref[i]).astype(bf16)
        return carry

    lax.fori_loop(0, n_rows, finish, 0)

    def wait_share(y):
        @pl.when(2 * y + half != col)
        def _():
            pltpu.make_async_copy(col_rx.at[y], col_rx.at[y], col_recv.at[0, y]).wait()

    over(0, 4, wait_share)
    share = jnp.zeros((72, 128), f32)
    for y in range(4):
        share = share + col_rx[y].astype(f32)
    share = share * factor
    share = jnp.concatenate([share[0:24], share[24:48], share[48:72]], axis=1)
    g_in_out_ref[...] = share[:, 0:channels].T
    g_out_out_ref[...] = share[:, channels : 2 * channels]

    gat_rx[place] = gat_tx[...]

    def wait_gather(step):
        peer = lax.rem(place + step, 16)
        pltpu.make_async_copy(gat_tx, gat_rx.at[peer], gat_recv.at[peer]).wait()

    over(1, 16, wait_gather)
    for j in range(16):
        up, across = 8 * (j // 2), 128 * (j % 2)
        score_rx[up : up + 8, across : across + 128] = gat_rx[j]
    for a in range(7):
        g_kernel_ref[a] = score_rx[7 * a : 7 * a + 7, 0:channels]
    g_rows_ref[...] = score_rx[48:56, 0:channels]
    picked = jnp.zeros((1, 256), f32)
    for k in range(4):
        picked = picked + jnp.where(row // 8 == k, score_rx[54 + k : 55 + k, :], 0.0)
    picked = pltpu.roll(
        jnp.broadcast_to(picked, (8, 256)), lax.rem(256 - SHARE * lax.rem(row, 8), 256), 1
    )
    g_bias_out_ref[...] = picked[0:1, 0:SHARE]

    halo_send(image_ref, halo, halo_sems, row, col, lambda copy: copy.wait_send())
    halo_send(d_block_ref, d_halo, d_halo_sems, row, col, lambda copy: copy.wait_send())
    over_rows(lambda j: row_copy(j).wait_send())
    over_rows(lambda j: s_row_copy(j).wait_send())

    @pl.when(owner)
    def _():
        over(1, 8, lambda step: col_copy(step).wait_send())
        over(1, 8, lambda step: s_col_copy(step).wait_send())

    over(1, 16, lambda step: gather_copy(step).wait_send())


def fused(image, cotangent, conv_kernel, rows, in_weight, out_weight, factor):
    n_rows, n_cols, channels = image.shape
    hidden_units = in_weight.shape[1]
    vmem = pl.BlockSpec(memory_space=pltpu.VMEM)
    dma = pltpu.SemaphoreType.DMA
    f32, bf16 = jnp.float32, jnp.bfloat16
    halo = [
        pltpu.VMEM((3, n_cols, channels), bf16),
        pltpu.VMEM((3, n_cols, channels), bf16),
        pltpu.VMEM((n_rows + 6, 16, channels), bf16),
        pltpu.VMEM((n_rows + 6, 16, channels), bf16),
    ]
    return pl.pallas_call(
        functools.partial(fused_kernel, factor),
        out_shape=(
            jax.ShapeDtypeStruct(image.shape, bf16),
            jax.ShapeDtypeStruct(image.shape, bf16),
            jax.ShapeDtypeStruct((7, 7, channels), f32),
            jax.ShapeDtypeStruct((8, channels), f32),
            jax.ShapeDtypeStruct((channels, SHARE), f32),
            jax.ShapeDtypeStruct((1, SHARE), f32),
            jax.ShapeDtypeStruct((SHARE, channels), f32),
        ),
        in_specs=[vmem] * 6,
        out_specs=(vmem,) * 7,
        scratch_shapes=[
            pltpu.VMEM((56, 256), f32),
            pltpu.VMEM((hidden_units, channels), bf16),
            pltpu.VMEM((channels, hidden_units), bf16),
            pltpu.VMEM((n_rows + 6, 200, 128), f32),
            pltpu.VMEM((n_rows + 6, 104, 128), f32),
            pltpu.VMEM((n_rows, n_cols, channels), f32),
            pltpu.VMEM((n_rows, n_cols, 128), f32),
            pltpu.VMEM((n_rows, n_cols // 2, 128), f32),
            pltpu.VMEM((n_rows, n_cols, channels), bf16),
            *halo,
            *halo,
            pltpu.VMEM((5, 8, channels), f32),
            pltpu.VMEM((49, 8, 256), f32),
            pltpu.VMEM((8, hidden_units), f32),
            pltpu.VMEM((channels, hidden_units), f32),
            pltpu.VMEM((channels, hidden_units), f32),
            pltpu.VMEM((hidden_units, 2 * channels), f32),
            pltpu.VMEM((64, 256), f32),
            pltpu.VMEM((16, 72, 128), bf16),
            pltpu.VMEM((16, 72, 128), bf16),
            pltpu.VMEM((64, 256), f32),
            pltpu.VMEM((16, 72, 128), bf16),
            pltpu.VMEM((16, 8, 128), f32),
            pltpu.VMEM((32, 72, 128), bf16),
            pltpu.VMEM((32, 8, 128), f32),
            pltpu.VMEM((4, 72, 128), bf16),
            pltpu.VMEM((4, 8, 128), f32),
            pltpu.VMEM((8, 128), f32),
            pltpu.VMEM((16, 8, 128), f32),
            dma((2, 8)),
            dma((2, 8)),
            dma((2,)),
            dma((2,)),
            dma((2, 16)),
            dma((2, 32)),
            dma((2, 8)),
            dma((2, 4)),
            dma((16,)),
            dma((16,)),
        ],
        compiler_params=pltpu.CompilerParams(
            collective_id=0, has_side_effects=True, vmem_limit_bytes=VMEM_LIMIT
        ),
    )(image, cotangent, conv_kernel, rows, in_weight, out_weight)


def body(
    image,
    conv_kernel,
    conv_bias,
    norm_gain,
    norm_bias,
    in_weight,
    in_bias,
    out_weight,
    out_bias,
    layer_scale,
    cotangent,
):
    n_rows, n_cols, channels = image.shape
    hidden_units = in_weight.shape[1]
    factor = 1.0 / math.sqrt(n_rows * lax.axis_size("rows") * n_cols * lax.axis_size("cols"))
    rows = jnp.stack([conv_bias, norm_gain, norm_bias, out_bias, layer_scale])
    rows = jnp.pad(rows, ((0, 0), (0, hidden_units - channels)))
    rows = jnp.concatenate([rows, in_bias[None], jnp.zeros((2, hidden_units), jnp.float32)], axis=0)
    output, grad_image, g_kernel, g_rows, g_in, g_bias, g_out = fused(
        image, cotangent, conv_kernel, rows, in_weight, out_weight, factor
    )
    return (
        output,
        grad_image,
        g_kernel,
        g_rows[1],
        g_rows[2],
        g_rows[3],
        g_in,
        g_bias[0],
        g_out,
        g_rows[4],
        g_rows[5],
    )


def solution(mesh):
    placed = (
        P("rows", "cols", None),
        P(),
        P(),
        P(),
        P(),
        P(),
        P(),
        P(),
        P(),
        P(),
        P("rows", "cols", None),
    )
    return jax.shard_map(
        body,
        mesh=mesh,
        in_specs=placed,
        out_specs=(
            P("rows", "cols", None),
            P("rows", "cols", None),
            P(),
            P(),
            P(),
            P(),
            P(None, "rows"),
            P("rows"),
            P("rows", None),
            P(),
            P(),
        ),
        check_vma=False,
    )
```

time: 618 us -> 96.1 us (0.16)
  waiting for transfers between devices: 235 us -> 0 us
  blocking collectives: 168 us -> 0 us
  other arithmetic: 119 us -> 0.68 us
  Pallas kernels: 0 us -> 82.3 us
  matrix products: 31.8 us -> 0 us
  starting transfers between devices: 21.9 us -> 0 us
  between operations: 16.3 us -> 0.67 us
  local copies, waits for them, and re-layouts: 24.9 us -> 12.2 us
    reduce_scatter x2 -> x0, waiting for transfers between devices: 229 us -> none  [the longest x1 219 us: body(): lax.psum_scatter(band_sums[2], 'rows', scatter_dimension=0, tiled=True)]
    psum x2 -> x0, blocking collectives: 111 us -> none  [the longest x1 83.3 us: body(): lax.psum((g_kernel, g_conv_bias, g_gain, g_norm_bias, g_out_bias, g_scale...]
    pallas_call x0 -> x1, Pallas kernels: none -> 82.3 us  [fused(): pl.pallas_call(functools.partial(fused_kernel, factor), out_shape=(jax.Sh...]
    reduce_sum x12 -> x0, other arithmetic: 74.4 us -> none  [the longest x8 35 us: partials(): tap_sums.append(jnp.sum(shifted * d_conv, axis=(0, 1)))]
    unnamed x1 -> x0, blocking collectives: 57.2 us -> none
    convert_element_type x2 -> x0, other arithmetic: 38 us -> none  [the longest x1 35.3 us: body(): grad_image = (cotangent.astype(jnp.float32) + transposed(d_padded, conv_k...]
    dot_general x6 -> x0, matrix products: 31.8 us -> none  [the longest x1 6.21 us: layer_pass(): lax.dot_general(d_hidden, in_weight, (((1,), (1,)), ((), ())), preferred_...]
    ppermute x8 -> x0, starting transfers between devices: 21.9 us -> none  [the longest x4 12.8 us: padded_2(): before = lax.ppermute(last, axis, up)]
  transfers between devices with their start and end apart: 10 -> 0, of which waited for: 5 -> 0; matrix products, arithmetic and copies ran while one was open for 10% -> 0% of each run, Pallas kernels for 0% -> 0%
where the time goes in v3:
time: 96.1 us; the launch traced here: 95.8 us
  Pallas kernels  82.3 us (86%)
  local copies, waits for them, and re-layouts  12.2 us (13%)
    pallas_call x1, Pallas kernels, fused(): pl.pallas_call(functools.partial(fused_kernel, factor), out_shape=(jax.Sh...  82.3 us
    unnamed x15, local copies, waits for them, and re-layouts  9.16 us

profile of v3, /device:TPU:1, one launch (start us, length us, event | category | flops | bytes accessed | tf_op | source)
XLA Modules:
  0.0 95.8 jit_solution(7913526152518628834)
XLA Ops:
  0.6 1.9 %copy.22.out_weight_ref = bf16[768,192]{1,0:T(8,128)(2,1)} copy(bf16[768,192]{0,1:T(8,128)(2,1)} %param.18) | data formatting | bytes 589824 | tf_op args[7]
  2.5 0.8 stack.23
  3.3 0.7 broadcast_in_dim.6
  4.0 0.1 pad.7.clone
  4.1 0.7 fusion.rows_ref
  4.7 82.3 %shard_map.194 = (bf16[16,192,192]{2,1,0:T(8,128)(2,1)}, bf16[16,192,192]{2,1,0:T(8,128)(2,1)}, f32[7,7,192]{2,1,0:T(8,128)}, f32[8,192]{1,0:T(8,128)}, f32[192,...) custom-call(bf16[16,192,192]{2,1,0:T(8,128)(2,1)} %image_ref.1, bf16[16,192,192]{2,1,0:T(8,128)(2,1)} %cot_ref.1, ...), custom_call_target="tpu_custom_call" | custom-call | tf_op jit(solution)/shard_map/pallas_call | solution.py:606
  87.1 1.5 %fusion.1 = (f32[1,192]{1,0:T(1,128)}, f32[1,192]{1,0:T(1,128)}, f32[1,192]{1,0:T(1,128)}, f32[1,192]{1,0:T(1,128)}, f32[1,192]{1,0:T(1,128)}) fusion(f32[8,192]{1,0:T(8,128)} %get-tuple-element.21), kind=kLoop, calls=%fused_computation.3 | loop fusion | bytes 7680 | tf_op jit(solution)/shard_map/slice | solution.py:699
  88.5 1.6 %copy.23 = f32[192,24]{0,1:T(8,128)} copy(f32[192,24]{1,0:T(8,128)} %get-tuple-element.31) | data formatting | bytes 36864
  90.1 0.0 copy-start
  90.1 2.8 %copy.29 = bf16[16,192,192]{2,1,0:T(8,128)(2,1)} copy(bf16[16,192,192]{2,1,0:T(8,128)(2,1)} %get-tuple-element.52) | data formatting | bytes 2359296
  92.9 0.0 copy-done
  92.9 0.0 copy-start.1
  92.9 0.0 copy-start.3
  92.9 0.0 copy-start.2
  92.9 1.1 %copy.30 = bf16[16,192,192]{2,1,0:T(8,128)(2,1)} copy(bf16[16,192,192]{2,1,0:T(8,128)(2,1)S(1)} %copy-done) | data formatting | bytes 2359296
  94.1 0.0 copy-done.1
  94.1 0.6 copy.31
  94.7 0.0 copy-done.3
  94.7 0.5 copy.32
  95.2 0.0 copy-done.2
  95.2 0.6 copy.33
  (1 shorter events, 0.0 us)
Async XLA Ops:
  90.1 2.8 %copy-start = (bf16[16,192,192]{2,1,0:T(8,128)(2,1)S(1)}, bf16[16,192,192]{2,1,0:T(8,128)(2,1)}, u32[]{:S(2)}) copy-start(bf16[16,192,192]{2,1,0:T(8,128)(2,1)} %get-tuple-element.53) | copy-start | bytes 3538948
  92.9 1.2 %copy-start.1 = (f32[7,7,192]{2,1,0:T(8,128)S(1)}, f32[7,7,192]{2,1,0:T(8,128)}, u32[]{:S(2)}) copy-start(f32[7,7,192]{2,1,0:T(8,128)} %get-tuple-element.54) | copy-start | bytes 112900
  92.9 1.8 %copy-start.3 = (f32[1,24]{1,0:T(1,128)S(1)}, f32[1,24]{1,0:T(1,128)}, u32[]{:S(2)}) copy-start(f32[1,24]{1,0:T(1,128)} %get-tuple-element.23) | copy-start | bytes 292
  92.9 2.3 %copy-start.2 = (f32[24,192]{1,0:T(8,128)S(1)}, f32[24,192]{1,0:T(8,128)}, u32[]{:S(2)}) copy-start(f32[24,192]{1,0:T(8,128)} %get-tuple-element.60) | copy-start | bytes 55300

commit v4 on v3

--- a/solution.py
+++ b/solution.py
@@ -18,7 +18,7 @@
 MESH = pl.DeviceIdType.MESH
 SHARE = 24
 CHUNK = 2
-VMEM_LIMIT = 64 * 1024 * 1024 - 65536
+VMEM_LIMIT = 50 * 1024 * 1024
 SIDES = ((-1, 0), (1, 0), (0, -1), (0, 1), (-1, -1), (-1, 1), (1, -1), (1, 1))
 
 
@@ -177,22 +177,106 @@
     lax.fori_loop(span[0], span[1], step, 0)
 
 
-def tap_sums(wide_ref, d_ref, first, sums_ref, steps):
-    n_rows = d_ref.shape[0]
-
+def split_taps(taps_ref, parts_ref, flip):
+    row = [taps_ref[7 * a : 7 * a + 7, :] for a in (range(6, -1, -1) if flip else range(7))]
+    groups = (
+        (row[0], row[2], row[4], row[6]),
+        (row[0] + row[1], row[2] + row[3], row[4] + row[5], row[6]),
+        (row[1], row[3], row[5], jnp.zeros_like(row[0])),
+    )
+    for g, taps in enumerate(groups):
+        for j in range(2):
+            even, odd = taps[2 * j], taps[2 * j + 1]
+            for q, part in enumerate((even, even + odd, odd)):
+                parts_ref[(3 * g + q) * 2 + j, 0:7] = part
+
+
+def split_rows(wide_ref, parts_ref):
+    def step(i, carry):
+        at = pl.ds(pl.multiple_of(8 * i, 8), 8)
+        x = [wide_ref[r, at, :] for r in range(22)]
+        groups = (
+            [x[2 * m] - x[2 * m + 1] for m in range(11)],
+            [x[2 * m + 1] for m in range(11)],
+            [x[2 * m + 2] - x[2 * m + 1] for m in range(10)],
+        )
+        for g, s in enumerate(groups):
+            for n in range(5):
+                parts_ref[15 * g + n, at, :] = s[2 * n] - s[2 * n + 1]
+                parts_ref[15 * g + 5 + n, at, :] = s[2 * n + 1]
+                if 2 * n + 2 < len(s):
+                    parts_ref[15 * g + 10 + n, at, :] = s[2 * n + 2] - s[2 * n + 1]
+        return carry
+
+    lax.fori_loop(0, wide_ref.shape[1] // 8, step, 0)
+
+
+def part_terms():
+    return [(g, q, j) for g in range(3) for q in range(3) for j in range(2) if (g, q, j) != (2, 2, 1)]
+
+
+def part_rows(parts_ref, start):
+    counts = [5] * 8 + [4]
+    return [parts_ref[5 * k : 5 * k + n, pl.ds(start, 8), :] for k, n in enumerate(counts)]
+
+
+def part_tile(parts_ref, taps_ref, first, start, flip):
+    accum = [None] * 9
+    for b in range(7):
+        rows = part_rows(parts_ref, start + b)
+        for g, q, j in part_terms():
+            k = 3 * g + q
+            tap = 6 - b if flip else b
+            term = rows[k][j : j + 4] * taps_ref[2 * k + j, tap : tap + 1, first : first + 128]
+            accum[k] = term if accum[k] is None else accum[k] + term
+    even = [accum[3 * g] + accum[3 * g + 1] for g in range(3)]
+    odd = [accum[3 * g + 1] + accum[3 * g + 2] for g in range(3)]
+    out = []
+    for n in range(4):
+        for p in (even, odd):
+            out.append(p[0][n : n + 1] + p[1][n : n + 1])
+            out.append(p[1][n : n + 1] + p[2][n : n + 1])
+    return jnp.concatenate(out, axis=0)
+
+
+def tap_sums(parts_ref, d_ref, first, sums_ref, steps):
     def step(i, carry):
         start = pl.multiple_of(8 * i, 8)
-        d_tile = d_ref[:, pl.ds(start, 8), :]
+        d = [d_ref[r, pl.ds(start, 8), :] for r in range(16)]
+        even, odd = d[0::2], d[1::2]
+        vectors = []
+        for v in (even, [a + b for a, b in zip(even, odd)], odd):
+            v_even, v_odd = v[0::2], v[1::2]
+            vectors += [v_even, [a + b for a, b in zip(v_even, v_odd)], v_odd]
+        vectors = [jnp.stack(v) for v in vectors]
         for b in range(7):
-            shifted = wide_ref[:, pl.ds(start + b, 8), :]
-            for a in range(7):
-                tap = 7 * a + b
-                sums_ref[tap, :, first : first + 128] += jnp.sum(
-                    shifted[a : a + n_rows] * d_tile, axis=0
-                )
+            dots = {}
+            rows = part_rows(parts_ref, start + b)
+            for g, q, j in part_terms():
+                k = 3 * g + q
+                dots[g, q, j] = jnp.sum(rows[k][j : j + 4] * vectors[k], axis=0)
+            p = {}
+            for g in range(3):
+                for j in range(2):
+                    p[g, 2 * j] = dots[g, 0, j] + dots[g, 1, j]
+                    if (g, j) != (2, 1):
+                        p[g, 2 * j + 1] = dots[g, 1, j] + dots[g, 2, j]
+            for i in range(4):
+                sums_ref[14 * i + b, :, first : first + 128] += p[0, i] + p[1, i]
+                if i < 3:
+                    sums_ref[14 * i + 7 + b, :, first : first + 128] += p[1, i] + p[2, i]
         return carry
 
     lax.fori_loop(0, steps, step, 0)
+
+
+def part_tiles(parts_ref, taps_ref, first, out_ref, put, span):
+    def step(i, carry):
+        start = pl.multiple_of(8 * i, 8)
+        put(out_ref, start, slice(0, 16), part_tile(parts_ref, taps_ref, first, start, True))
+        return carry
+
+    lax.fori_loop(span[0], span[1], step, 0)
 
 
 def fold(values):
@@ -202,11 +286,16 @@
 def fused_kernel(
     factor,
     image_ref,
-    cot_ref,
+    cot_hbm_ref,
     kernel_ref,
-    rows_ref,
+    conv_bias_ref,
+    gain_ref,
+    norm_bias_ref,
+    out_bias_ref,
+    layer_scale_ref,
+    in_bias_ref,
     in_weight_ref,
-    out_weight_ref,
+    out_t_ref,
     output_ref,
     grad_image_ref,
     g_kernel_ref,
@@ -214,11 +303,15 @@
     g_in_out_ref,
     g_bias_out_ref,
     g_out_out_ref,
+    cot_ref,
     taps_ref,
     in_t_ref,
-    out_t_ref,
+    out_weight_ref,
     main_ref,
     rest_ref,
+    pmain_ref,
+    prest_ref,
+    ptaps_ref,
     conv_ref,
     d_main_ref,
     d_rest_ref,
@@ -259,6 +352,7 @@
     col_recv,
     gat_send,
     gat_recv,
+    cot_sem,
 ):
     n_rows, n_cols, channels = image_ref.shape
     pixels = CHUNK * n_cols
@@ -274,6 +368,8 @@
     halo = (top_ref, bottom_ref, left_ref, right_ref)
     d_halo = (d_top_ref, d_bottom_ref, d_left_ref, d_right_ref)
 
+    cot_copy = pltpu.make_async_copy(cot_hbm_ref, cot_ref, cot_sem)
+    cot_copy.start()
     barrier = pltpu.get_barrier_semaphore()
 
     def greet_row(step, carry):
@@ -304,13 +400,14 @@
     halo_send(image_ref, halo, halo_sems, row, col, lambda copy: copy.start())
     tiles(main_ref, taps_ref, 0, False, conv_ref, put_main, own, (1, 23))
     in_t_ref[...] = in_weight_ref[...].astype(f32).T.astype(bf16)
-    out_t_ref[...] = out_weight_ref[...].astype(f32).T.astype(bf16)
+    out_weight_ref[...] = out_t_ref[...].astype(f32).T.astype(bf16)
     sums_ref[...] = jnp.zeros_like(sums_ref)
     tap_ref[...] = jnp.zeros_like(tap_ref)
     bias_sum_ref[...] = jnp.zeros_like(bias_sum_ref)
     g_in_ref[...] = jnp.zeros_like(g_in_ref)
     g_out_ref[...] = jnp.zeros_like(g_out_ref)
     s_ref[...] = jnp.zeros_like(s_ref)
+    cot_copy.wait()
     halo_wait(image_ref, halo, halo_sems, row, col)
 
     def widen_all(block_ref, pieces, center):
@@ -327,17 +424,20 @@
     tiles(main_ref, taps_ref, 0, False, conv_ref, put_main, whole, (0, 2), 23)
     tiles(rest_ref, taps_ref, 128, False, conv_ref, put_rest, whole, (0, 2), 11)
 
+    split_taps(taps_ref, ptaps_ref, True)
+    split_rows(main_ref, pmain_ref)
+    split_rows(rest_ref, prest_ref)
+
     def chunk(i, carry):
         span = pl.ds(CHUNK * i, CHUNK)
-        conv_bias, gain, norm_bias, out_bias, layer_scale = (
-            rows_ref[k : k + 1, 0:channels] for k in range(5)
-        )
+        conv_bias, gain, norm_bias = conv_bias_ref[...], gain_ref[...], norm_bias_ref[...]
+        out_bias, layer_scale = out_bias_ref[...], layer_scale_ref[...]
         conv_out = conv_ref[span].reshape(pixels, channels) + conv_bias
         centred = conv_out - jnp.mean(conv_out, axis=-1, keepdims=True)
         inv_std = lax.rsqrt(jnp.mean(centred * centred, axis=-1, keepdims=True) + 1e-06)
         unit_norm = centred * inv_std
         normed = (unit_norm * gain + norm_bias).astype(bf16)
-        hidden = jnp.dot(normed, in_weight_ref[...], preferred_element_type=f32) + rows_ref[5:6]
+        hidden = jnp.dot(normed, in_weight_ref[...], preferred_element_type=f32) + in_bias_ref[...]
         act_full, gelu_slope = gelu_parts(hidden)
         activation = act_full.astype(bf16)
         branch = jnp.dot(activation, out_weight_ref[...], preferred_element_type=f32) + out_bias
@@ -393,7 +493,7 @@
     to_core_s = remote(s_ref, score_rx, core_send.at[1], core_recv.at[1], (row, other))
     to_core.start()
 
-    tap_sums(rest_ref, d_rest_ref, 128, tap_ref, 12)
+    tap_sums(prest_ref, d_rest_ref, 128, tap_ref, 12)
     to_core.wait()
 
     def row_copy(j):
@@ -464,12 +564,12 @@
     lax.fori_loop(0, 16, pack_row, 0)
     over_rows(lambda j: row_copy(j).start())
 
-    tap_sums(main_ref, d_main_ref, 0, tap_ref, 24)
+    tap_sums(pmain_ref, d_main_ref, 0, tap_ref, 24)
     taps = jnp.sum(tap_ref[...], axis=1)
     s_ref[0:49, 0:128] = taps[:, 0:128]
     s_ref[0:49, 128:192] = taps[:, 128:192] + taps[:, 192:256]
     s_ref[49:54, 0:channels] = jnp.sum(sums_ref[...], axis=1)
-    s_ref[52:53, 0:channels] = s_ref[52:53, 0:channels] * rows_ref[4:5, 0:channels]
+    s_ref[52:53, 0:channels] = s_ref[52:53, 0:channels] * layer_scale_ref[...]
     bias_sum = jnp.sum(bias_sum_ref[...], axis=0, keepdims=True)
     for k in range(4):
         s_ref[54 + k : 55 + k, 0:channels] = bias_sum[:, channels * k : channels * (k + 1)]
@@ -477,7 +577,9 @@
 
     halo_wait(d_block_ref, d_halo, d_halo_sems, row, col)
     widen_all(d_block_ref, d_halo, True)
-    tiles(rest_ref, taps_ref, 128, True, conv_ref, put_rest, whole, (0, 6))
+    split_rows(main_ref, pmain_ref)
+    split_rows(rest_ref, prest_ref)
+    part_tiles(prest_ref, ptaps_ref, 128, conv_ref, put_rest, (0, 6))
 
     to_core_s.wait()
     for j in range(16):
@@ -505,7 +607,7 @@
         col_rx[col // 2] = total.astype(bf16)
         over(1, 8, lambda step: col_copy(step).start())
 
-    tiles(main_ref, taps_ref, 0, True, conv_ref, put_main, whole, (0, 12))
+    part_tiles(pmain_ref, ptaps_ref, 0, conv_ref, put_main, (0, 12))
 
     @pl.when(owner)
     def _():
@@ -523,7 +625,7 @@
         scol_rx[col // 2] = lax.fori_loop(0, 32, add_row, jnp.zeros((8, 128), f32))
         over(1, 8, lambda step: s_col_copy(step).start())
 
-    tiles(main_ref, taps_ref, 0, True, conv_ref, put_main, whole, (12, 18))
+    part_tiles(pmain_ref, ptaps_ref, 0, conv_ref, put_main, (12, 18))
 
     def wait_col(y):
         @pl.when(2 * y + half != col)
@@ -534,8 +636,8 @@
     gat_tx[...] = ((scol_rx[0] + scol_rx[1]) + (scol_rx[2] + scol_rx[3])) * factor
     over(1, 16, lambda step: gather_copy(step).start())
 
-    tiles(main_ref, taps_ref, 0, True, conv_ref, put_main, whole, (18, 24))
-    tiles(rest_ref, taps_ref, 128, True, conv_ref, put_rest, whole, (6, 12))
+    part_tiles(pmain_ref, ptaps_ref, 0, conv_ref, put_main, (18, 24))
+    part_tiles(prest_ref, ptaps_ref, 128, conv_ref, put_rest, (6, 12))
 
     def finish(i, carry):
         grad_image_ref[i] = (cot_ref[i].astype(f32) + conv_ref[i]).astype(bf16)
@@ -554,7 +656,7 @@
         share = share + col_rx[y].astype(f32)
     share = share * factor
     share = jnp.concatenate([share[0:24], share[24:48], share[48:72]], axis=1)
-    g_in_out_ref[...] = share[:, 0:channels].T
+    g_in_out_ref[...] = share[:, 0:channels]
     g_out_out_ref[...] = share[:, channels : 2 * channels]
 
     gat_rx[place] = gat_tx[...]
@@ -591,7 +693,7 @@
     over(1, 16, lambda step: gather_copy(step).wait_send())
 
 
-def fused(image, cotangent, conv_kernel, rows, in_weight, out_weight, factor):
+def fused(image, cotangent, conv_kernel, vectors, in_weight, out_weight_t, factor):
     n_rows, n_cols, channels = image.shape
     hidden_units = in_weight.shape[1]
     vmem = pl.BlockSpec(memory_space=pltpu.VMEM)
@@ -610,18 +712,22 @@
             jax.ShapeDtypeStruct(image.shape, bf16),
             jax.ShapeDtypeStruct((7, 7, channels), f32),
             jax.ShapeDtypeStruct((8, channels), f32),
-            jax.ShapeDtypeStruct((channels, SHARE), f32),
+            jax.ShapeDtypeStruct((SHARE, channels), f32),
             jax.ShapeDtypeStruct((1, SHARE), f32),
             jax.ShapeDtypeStruct((SHARE, channels), f32),
         ),
-        in_specs=[vmem] * 6,
+        in_specs=[vmem, pl.BlockSpec(memory_space=pl.ANY)] + [vmem] * 9,
         out_specs=(vmem,) * 7,
         scratch_shapes=[
+            pltpu.VMEM(image.shape, bf16),
             pltpu.VMEM((56, 256), f32),
             pltpu.VMEM((hidden_units, channels), bf16),
-            pltpu.VMEM((channels, hidden_units), bf16),
+            pltpu.VMEM((hidden_units, channels), bf16),
             pltpu.VMEM((n_rows + 6, 200, 128), f32),
             pltpu.VMEM((n_rows + 6, 104, 128), f32),
+            pltpu.VMEM((45, 200, 128), f32),
+            pltpu.VMEM((45, 104, 128), f32),
+            pltpu.VMEM((18, 8, 256), f32),
             pltpu.VMEM((n_rows, n_cols, channels), f32),
             pltpu.VMEM((n_rows, n_cols, 128), f32),
             pltpu.VMEM((n_rows, n_cols // 2, 128), f32),
@@ -656,11 +762,12 @@
             dma((2, 4)),
             dma((16,)),
             dma((16,)),
+            dma,
         ],
         compiler_params=pltpu.CompilerParams(
             collective_id=0, has_side_effects=True, vmem_limit_bytes=VMEM_LIMIT
         ),
-    )(image, cotangent, conv_kernel, rows, in_weight, out_weight)
+    )(image, cotangent, conv_kernel, *vectors, in_weight, out_weight_t)
 
 
 def body(
@@ -676,14 +783,12 @@
     layer_scale,
     cotangent,
 ):
-    n_rows, n_cols, channels = image.shape
-    hidden_units = in_weight.shape[1]
+    n_rows, n_cols, _ = image.shape
     factor = 1.0 / math.sqrt(n_rows * lax.axis_size("rows") * n_cols * lax.axis_size("cols"))
-    rows = jnp.stack([conv_bias, norm_gain, norm_bias, out_bias, layer_scale])
-    rows = jnp.pad(rows, ((0, 0), (0, hidden_units - channels)))
-    rows = jnp.concatenate([rows, in_bias[None], jnp.zeros((2, hidden_units), jnp.float32)], axis=0)
+    vectors = (conv_bias, norm_gain, norm_bias, out_bias, layer_scale, in_bias)
+    vectors = [vector[None] for vector in vectors]
     output, grad_image, g_kernel, g_rows, g_in, g_bias, g_out = fused(
-        image, cotangent, conv_kernel, rows, in_weight, out_weight, factor
+        image, cotangent, conv_kernel, vectors, in_weight, out_weight.T, factor
     )
     return (
         output,
@@ -692,7 +797,7 @@
         g_rows[1],
         g_rows[2],
         g_rows[3],
-        g_in,
+        g_in.T,
         g_bias[0],
         g_out,
         g_rows[4],

time: 96.1 us -> 94 us (0.978)
  Pallas kernels: 82.3 us -> 80.9 us
    unnamed x15 -> x22, local copies, waits for them, and re-layouts: 9.16 us -> 10.8 us
    pallas_call x1, Pallas kernels: 82.3 us -> 80.9 us  [fused(): pl.pallas_call(functools.partial(fused_kernel, factor), out_shape=(jax.Sh...]
where the time goes in v4:
time: 94 us; the launch traced here: 93.6 us
  Pallas kernels  80.9 us (86%)
  local copies, waits for them, and re-layouts  12 us (13%)
    pallas_call x1, Pallas kernels, fused(): pl.pallas_call(functools.partial(fused_kernel, factor), out_shape=(jax.Sh...  80.9 us
    unnamed x22, local copies, waits for them, and re-layouts  10.8 us

profile of v4, /device:TPU:1, one launch (start us, length us, event | category | flops | bytes accessed | tf_op | source)
XLA Modules:
  0.0 93.6 jit_solution(2759609625121173289)
XLA Ops:
  0.6 0.7 broadcast_in_dim.23.in_bias_ref
  1.3 0.0 copy-start
  1.3 1.0 %copy-done = bf16[192,768]{1,0:T(8,128)(2,1)S(1)} copy-done((bf16[192,768]{1,0:T(8,128)(2,1)S(1)}, bf16[192,768]{1,0:T(8,128)(2,1)}, u32[]{:S(2)}) %copy-start) | copy-done | bytes 294936
  2.3 0.0 copy-start.1
  2.3 1.0 %copy-done.1 = bf16[768,192]{0,1:T(8,128)(2,1)S(1)} copy-done((bf16[768,192]{0,1:T(8,128)(2,1)S(1)}, bf16[768,192]{0,1:T(8,128)(2,1)}, u32[]{:S(2)}) %copy-start.1) | copy-done | bytes 294936
  3.3 0.0 copy-start.2
  3.3 0.8 copy-done.2
  4.1 0.0 copy-start.3
  4.1 0.7 copy-done.3
  4.8 0.0 copy-start.4
  4.8 0.7 copy-done.4
  5.4 0.0 copy-start.5
  5.4 0.7 copy-done.5
  6.1 0.0 copy-start.6
  6.1 0.7 copy-done.6
  6.8 0.0 copy-start.7
  6.8 0.7 copy-done.7
  7.5 80.9 %shard_map.194 = (bf16[16,192,192]{2,1,0:T(8,128)(2,1)S(1)}, bf16[16,192,192]{2,1,0:T(8,128)(2,1)S(1)}, f32[7,7,192]{2,1,0:T(8,128)S(1)}, f32[8,192]{1,0:T(8,128...) custom-call(bf16[16,192,192]{2,1,0:T(8,128)(2,1)} %image_ref.1, ...), custom_call_target="tpu_custom_call" | custom-call | tf_op jit(solution)/shard_map/pallas_call | solution.py:708
  88.4 0.6 fusion
  89.0 1.1 %copy.28 = bf16[16,192,192]{2,1,0:T(8,128)(2,1)} copy(bf16[16,192,192]{2,1,0:T(8,128)(2,1)S(1)} %get-tuple-element.41) | data formatting | bytes 2359296
  90.1 1.1 %copy.29 = bf16[16,192,192]{2,1,0:T(8,128)(2,1)} copy(bf16[16,192,192]{2,1,0:T(8,128)(2,1)S(1)} %get-tuple-element.42) | data formatting | bytes 2359296
  91.3 0.6 copy.30
  91.9 0.6 copy.31
  92.5 0.5 copy.32
  93.0 0.6 copy.33
Async XLA Ops:
  1.3 1.0 %copy-start = (bf16[192,768]{1,0:T(8,128)(2,1)S(1)}, bf16[192,768]{1,0:T(8,128)(2,1)}, u32[]{:S(2)}) copy-start(bf16[192,768]{1,0:T(8,128)(2,1)} %in_weight_ref.1) | copy-start | bytes 884740
  2.3 1.0 %copy-start.1 = (bf16[768,192]{0,1:T(8,128)(2,1)S(1)}, bf16[768,192]{0,1:T(8,128)(2,1)}, u32[]{:S(2)}) copy-start(bf16[768,192]{0,1:T(8,128)(2,1)} %param.18) | copy-start | bytes 884740
  3.3 0.8 copy-start.2
  4.1 0.7 copy-start.3
  4.8 0.7 copy-start.4
  5.4 0.7 copy-start.5
  6.1 0.7 copy-start.6
  6.8 0.7 copy-start.7
